TPU v7x, 32 devices: a whole 2x2x4 slice. The times are simulated.
32 devices in a mesh: span: 2 (over y), tmpl: 2 (over x), stn: 8 (over z, core).
Axes of the slice: x: 2, y: 2, z: 4, core: 2. Of those that a mesh axis runs over, the one named last changes fastest.
Arguments:
- signal: bfloat16 [3072, 8192], P('stn', ('span', 'tmpl')), parts along dimension 1, may hold values from -110 to 110
- waveforms: bfloat16 [16, 4, 8, 300], P('tmpl'), may hold values from -40 to 40
- station_groups: int32 [16, 4], P('tmpl'), may hold values from 0 to 7, all different within a row; in each aligned block of 8 rows (0 to 7, 8 to 15, ...) at most 8 rows name the same one
- channel_offsets: int32 [16, 4, 8], P('tmpl'), may hold values from 0 to 383
- moveouts: int32 [16, 4, 8], P('tmpl'), may hold values from 0 to 639
Outputs:
- stack: float32 [16, 6144], P(('tmpl', 'stn'), 'span'), parts along dimension 1
There are 2 independent parts, one for each index of `span`. A program takes and returns all parts, laid end to end along the dimension named above; an argument that names none is the same for every part. Nothing has to cross between parts.
Inputs may be any that keep to these rules, and one draw needn't show every extreme that they name: `station_groups`: A template's 4 station groups are distinct. Among the 8 templates of one index of tmpl, at most 8 touch any one station group, and in every draw some station group is touched by exactly 8 of them.
All inputs are finite; a program needn't handle non-finite values.
Results may differ from a plain program's by a relative error of at most 0.0003.
Values may be sent and summed in bfloat16 or wider, within the bound.
No kernel may reach another device: no remote copies, remote signals or barrier semaphores. Data moves between devices by JAX's collectives and lax.ppermute only.
A program may use at most 64 MiB of HBM per device.

v0:
```python
import jax
import jax.numpy as jnp
from jax import lax
from jax.sharding import PartitionSpec as P

L = 300
NT = 3072


eps_value = 1e-05


def toeplitz_tiles(wave):
    length = wave.shape[0]
    padded = jnp.concatenate(
        [jnp.zeros((128,), wave.dtype), wave, jnp.zeros((513 - length,), wave.dtype)]
    )
    repeated = jnp.tile(padded, 128)[: 128 * 640].reshape(128, 640)
    return repeated[:, 128:640]


def entry_stack(wave_rows, chan_rows, move_rows, series, rms_data):
    toeplitz = jax.vmap(toeplitz_tiles)(wave_rows)
    blocks = NT // 128

    def one_slot(channel, lag_shift):
        data_row = lax.dynamic_slice(series, (channel, lag_shift), (1, NT + 384))
        energy = lax.dynamic_slice(rms_data, (channel, lag_shift), (1, NT))
        return (data_row.reshape(blocks + 3, 128), energy.reshape(NT))

    segments, scales = jax.vmap(one_slot)(chan_rows, move_rows)
    correl = jnp.zeros((wave_rows.shape[0], blocks, 128), jnp.float32)
    for offset in range(4):
        correl = correl + jnp.einsum(
            "pac,pbc->pab",
            segments[:, offset : offset + blocks],
            toeplitz[:, :, offset * 128 : (offset + 1) * 128],
            preferred_element_type=jnp.float32,
        )
    waves_wide = wave_rows.astype(jnp.float32)
    wave_rms = jnp.sqrt(jnp.mean(waves_wide * waves_wide, axis=1) + eps_value)
    normed = correl.reshape(wave_rows.shape[0], NT) / (L * wave_rms[:, None] * scales)
    return jnp.sum(normed, axis=0)


def add_sources(received):
    return jnp.sum(received, axis=0)


def shards(signal, waveforms, station_groups, channel_offsets, moveouts):
    series = lax.all_gather(signal, "tmpl", axis=1, tiled=True)
    group_rows = waveforms.shape[0]
    touch_count = station_groups.shape[1]
    station_count = lax.axis_size("stn")
    own_rows = group_rows // station_count
    capacity = min(group_rows, 2 * group_rows * touch_count // station_count)
    station = lax.axis_index("stn")
    is_local = station_groups == station
    present = jnp.any(is_local, axis=1)
    touch_pick = jnp.sum(
        is_local.astype(jnp.int32) * jnp.arange(touch_count, dtype=jnp.int32)[None, :], axis=1
    )
    position = jnp.cumsum(present.astype(jnp.int32)) - 1
    target = jnp.where(present, position, capacity)
    entry_tpl = (
        jnp.zeros((capacity,), jnp.int32)
        .at[target]
        .set(jnp.arange(group_rows, dtype=jnp.int32), mode="drop")
    )
    entry_touch = touch_pick[entry_tpl]
    live_count = jnp.sum(present.astype(jnp.int32))
    is_live = jnp.arange(capacity, dtype=jnp.int32) < live_count
    wave_sel = waveforms[entry_tpl, entry_touch]
    chan_sel = channel_offsets[entry_tpl, entry_touch]
    move_sel = moveouts[entry_tpl, entry_touch]
    wide_series = series.astype(jnp.float32)
    squares = wide_series * wide_series
    running = jnp.concatenate(
        [jnp.zeros((series.shape[0], 1), jnp.float32), jnp.cumsum(squares, axis=1)], axis=1
    )
    windows = running[:, L:] - running[:, :-L]
    rms_data = jnp.sqrt(windows / L + eps_value)

    def run_entry(entry_num):
        stacked = entry_stack(
            wave_sel[entry_num], chan_sel[entry_num], move_sel[entry_num], series, rms_data
        )
        return jnp.where(is_live[entry_num], stacked, 0.0)

    stacks = lax.map(run_entry, jnp.arange(capacity, dtype=jnp.int32))
    partial_sum = jnp.zeros((group_rows, NT), jnp.float32).at[entry_tpl].add(stacks)
    by_owner = partial_sum.reshape(station_count, own_rows, NT)
    return add_sources(lax.all_to_all(by_owner, "stn", split_axis=0, concat_axis=0, tiled=True))


def solution(mesh):
    in_specs = (
        P("stn", ("span", "tmpl")),
        P("tmpl", None, None, None),
        P("tmpl", None),
        P("tmpl", None, None),
        P("tmpl", None, None),
    )
    out_specs = P(("tmpl", "stn"), "span")
    return jax.shard_map(shards, mesh=mesh, in_specs=in_specs, out_specs=out_specs, check_vma=False)
```

profile of v0, /device:TPU:0, one launch (start us, length us, event | category | flops | bytes accessed | tf_op | source)
XLA Modules:
  0.0 578.0 jit_solution(9084490409785776008)
XLA Ops:
  14.1 42.4 %all-gather.2.cloned.1.call-done = bf16[384,4096]{1,0:T(8,128)(2,1)} async-done(((bf16[384,2048]{1,0:T(8,128)(2,1)}), bf16[384,4096]{1,0:T(8,128)(2,1)}) %all-gather.2.cloned.1.call-update) | async-done | bytes 3145744 | tf_op jit(solution)/shard_map/all_gather | solution.py:51
  59.2 3.9 copy.30
  63.1 6.7 %copy.20 = f32[384,32,128]{0,1,2:T(8,128)} copy(f32[384,32,128]{2,1,0:T(8,128)} %bitcast.101) | data formatting | bytes 12582912 | tf_op jit(solution)/shard_map/reshape.2
  79.3 3.6 copy.21
  83.0 5.2 fusion.16
  88.1 6.5 %copy.22 = f32[384,3797]{1,0:T(8,128)} copy(f32[384,3797]{0,1:T(8,128)} %fusion.16) | data formatting | bytes 11664384 | tf_op jit(solution)/shard_map/while | solution.py:90
  94.6 464.3 %while.21 = (s32[]{:T(128)}, f32[8,3072]{1,0:T(8,128)S(1)}, s32[8]{0:T(128)S(1)}, pred[8]{0:T(512)(128)(4,1)S(1)}, s32[8,8]{1,0:T(8,128)S(1)}, /*index=5*/s32[8,...) while((s32[]{:T(128)}, f32[8,3072]{1,0:T(8,128)S(1)}, ...), condition=%wide.region_10.11_spmd.clone, body=%wide.region_7.10_spmd.sunk.clone | while | flops 25351368 | bytes 14289844 | solution.py:90
  97.4 24.5 %while.19 = (s32[]{:T(128)}, bf16[384,4096]{1,0:T(8,128)(2,1)}, s32[8,2]{0,1:T(2,128)S(1)}, bf16[8,1,3456]{2,0,1:T(8,128)(2,1)S(1)}, s32[]{:T(128)}, /*index=5*/s32[]{:T(128)}) while((s32[]{:T(128)}, bf16[384,4096]{1,0:T(8,128)(2,1)}, s32[8,2]{0,1:T(2,128)S(1)}, bf16[8,1,3456]{2,0,1:T(8,128)(2,1)S(1)}, s32[]{:T(128)}, /*index=5*/s32[]{:T(128)}) %tuple.81), condition=%wide.while_cond, body=%wide.while_body.sunk | while | flops 2 | bytes 27765 | solution.py:27
  127.1 23.6 %while.20 = (s32[]{:T(128)}, f32[384,3797]{1,0:T(8,128)}, s32[8,2]{0,1:T(2,128)S(1)}, f32[8,1,3072]{2,1,0:T(1,128)S(1)}, s32[]{:T(128)}) while((s32[]{:T(128)}, f32[384,3797]{1,0:T(8,128)}, s32[8,2]{0,1:T(2,128)S(1)}, f32[8,1,3072]{2,1,0:T(1,128)S(1)}, s32[]{:T(128)}) %tuple.84), condition=%wide.while_cond.1, body=%wide.while_body.1.sunk | while | flops 2 | bytes 24685 | solution.py:28
  155.5 24.5 %while.19 = (s32[]{:T(128)}, bf16[384,4096]{1,0:T(8,128)(2,1)}, s32[8,2]{0,1:T(2,128)S(1)}, bf16[8,1,3456]{2,0,1:T(8,128)(2,1)S(1)}, s32[]{:T(128)}, /*index=5*/s32[]{:T(128)}) while((s32[]{:T(128)}, bf16[384,4096]{1,0:T(8,128)(2,1)}, s32[8,2]{0,1:T(2,128)S(1)}, bf16[8,1,3456]{2,0,1:T(8,128)(2,1)S(1)}, s32[]{:T(128)}, /*index=5*/s32[]{:T(128)}) %tuple.81), condition=%wide.while_cond, body=%wide.while_body.sunk | while | flops 2 | bytes 27765 | solution.py:27
  185.1 23.6 %while.20 = (s32[]{:T(128)}, f32[384,3797]{1,0:T(8,128)}, s32[8,2]{0,1:T(2,128)S(1)}, f32[8,1,3072]{2,1,0:T(1,128)S(1)}, s32[]{:T(128)}) while((s32[]{:T(128)}, f32[384,3797]{1,0:T(8,128)}, s32[8,2]{0,1:T(2,128)S(1)}, f32[8,1,3072]{2,1,0:T(1,128)S(1)}, s32[]{:T(128)}) %tuple.84), condition=%wide.while_cond.1, body=%wide.while_body.1.sunk | while | flops 2 | bytes 24685 | solution.py:28
  213.5 24.5 %while.19 = (s32[]{:T(128)}, bf16[384,4096]{1,0:T(8,128)(2,1)}, s32[8,2]{0,1:T(2,128)S(1)}, bf16[8,1,3456]{2,0,1:T(8,128)(2,1)S(1)}, s32[]{:T(128)}, /*index=5*/s32[]{:T(128)}) while((s32[]{:T(128)}, bf16[384,4096]{1,0:T(8,128)(2,1)}, s32[8,2]{0,1:T(2,128)S(1)}, bf16[8,1,3456]{2,0,1:T(8,128)(2,1)S(1)}, s32[]{:T(128)}, /*index=5*/s32[]{:T(128)}) %tuple.81), condition=%wide.while_cond, body=%wide.while_body.sunk | while | flops 2 | bytes 27765 | solution.py:27
  243.2 23.6 %while.20 = (s32[]{:T(128)}, f32[384,3797]{1,0:T(8,128)}, s32[8,2]{0,1:T(2,128)S(1)}, f32[8,1,3072]{2,1,0:T(1,128)S(1)}, s32[]{:T(128)}) while((s32[]{:T(128)}, f32[384,3797]{1,0:T(8,128)}, s32[8,2]{0,1:T(2,128)S(1)}, f32[8,1,3072]{2,1,0:T(1,128)S(1)}, s32[]{:T(128)}) %tuple.84), condition=%wide.while_cond.1, body=%wide.while_body.1.sunk | while | flops 2 | bytes 24685 | solution.py:28
  271.5 24.5 %while.19 = (s32[]{:T(128)}, bf16[384,4096]{1,0:T(8,128)(2,1)}, s32[8,2]{0,1:T(2,128)S(1)}, bf16[8,1,3456]{2,0,1:T(8,128)(2,1)S(1)}, s32[]{:T(128)}, /*index=5*/s32[]{:T(128)}) while((s32[]{:T(128)}, bf16[384,4096]{1,0:T(8,128)(2,1)}, s32[8,2]{0,1:T(2,128)S(1)}, bf16[8,1,3456]{2,0,1:T(8,128)(2,1)S(1)}, s32[]{:T(128)}, /*index=5*/s32[]{:T(128)}) %tuple.81), condition=%wide.while_cond, body=%wide.while_body.sunk | while | flops 2 | bytes 27765 | solution.py:27
  301.2 23.6 %while.20 = (s32[]{:T(128)}, f32[384,3797]{1,0:T(8,128)}, s32[8,2]{0,1:T(2,128)S(1)}, f32[8,1,3072]{2,1,0:T(1,128)S(1)}, s32[]{:T(128)}) while((s32[]{:T(128)}, f32[384,3797]{1,0:T(8,128)}, s32[8,2]{0,1:T(2,128)S(1)}, f32[8,1,3072]{2,1,0:T(1,128)S(1)}, s32[]{:T(128)}) %tuple.84), condition=%wide.while_cond.1, body=%wide.while_body.1.sunk | while | flops 2 | bytes 24685 | solution.py:28
  329.6 24.5 %while.19 = (s32[]{:T(128)}, bf16[384,4096]{1,0:T(8,128)(2,1)}, s32[8,2]{0,1:T(2,128)S(1)}, bf16[8,1,3456]{2,0,1:T(8,128)(2,1)S(1)}, s32[]{:T(128)}, /*index=5*/s32[]{:T(128)}) while((s32[]{:T(128)}, bf16[384,4096]{1,0:T(8,128)(2,1)}, s32[8,2]{0,1:T(2,128)S(1)}, bf16[8,1,3456]{2,0,1:T(8,128)(2,1)S(1)}, s32[]{:T(128)}, /*index=5*/s32[]{:T(128)}) %tuple.81), condition=%wide.while_cond, body=%wide.while_body.sunk | while | flops 2 | bytes 27765 | solution.py:27
  359.3 23.6 %while.20 = (s32[]{:T(128)}, f32[384,3797]{1,0:T(8,128)}, s32[8,2]{0,1:T(2,128)S(1)}, f32[8,1,3072]{2,1,0:T(1,128)S(1)}, s32[]{:T(128)}) while((s32[]{:T(128)}, f32[384,3797]{1,0:T(8,128)}, s32[8,2]{0,1:T(2,128)S(1)}, f32[8,1,3072]{2,1,0:T(1,128)S(1)}, s32[]{:T(128)}) %tuple.84), condition=%wide.while_cond.1, body=%wide.while_body.1.sunk | while | flops 2 | bytes 24685 | solution.py:28
  387.6 24.5 %while.19 = (s32[]{:T(128)}, bf16[384,4096]{1,0:T(8,128)(2,1)}, s32[8,2]{0,1:T(2,128)S(1)}, bf16[8,1,3456]{2,0,1:T(8,128)(2,1)S(1)}, s32[]{:T(128)}, /*index=5*/s32[]{:T(128)}) while((s32[]{:T(128)}, bf16[384,4096]{1,0:T(8,128)(2,1)}, s32[8,2]{0,1:T(2,128)S(1)}, bf16[8,1,3456]{2,0,1:T(8,128)(2,1)S(1)}, s32[]{:T(128)}, /*index=5*/s32[]{:T(128)}) %tuple.81), condition=%wide.while_cond, body=%wide.while_body.sunk | while | flops 2 | bytes 27765 | solution.py:27
  417.3 23.6 %while.20 = (s32[]{:T(128)}, f32[384,3797]{1,0:T(8,128)}, s32[8,2]{0,1:T(2,128)S(1)}, f32[8,1,3072]{2,1,0:T(1,128)S(1)}, s32[]{:T(128)}) while((s32[]{:T(128)}, f32[384,3797]{1,0:T(8,128)}, s32[8,2]{0,1:T(2,128)S(1)}, f32[8,1,3072]{2,1,0:T(1,128)S(1)}, s32[]{:T(128)}) %tuple.84), condition=%wide.while_cond.1, body=%wide.while_body.1.sunk | while | flops 2 | bytes 24685 | solution.py:28
  445.7 24.5 %while.19 = (s32[]{:T(128)}, bf16[384,4096]{1,0:T(8,128)(2,1)}, s32[8,2]{0,1:T(2,128)S(1)}, bf16[8,1,3456]{2,0,1:T(8,128)(2,1)S(1)}, s32[]{:T(128)}, /*index=5*/s32[]{:T(128)}) while((s32[]{:T(128)}, bf16[384,4096]{1,0:T(8,128)(2,1)}, s32[8,2]{0,1:T(2,128)S(1)}, bf16[8,1,3456]{2,0,1:T(8,128)(2,1)S(1)}, s32[]{:T(128)}, /*index=5*/s32[]{:T(128)}) %tuple.81), condition=%wide.while_cond, body=%wide.while_body.sunk | while | flops 2 | bytes 27765 | solution.py:27
  475.3 23.6 %while.20 = (s32[]{:T(128)}, f32[384,3797]{1,0:T(8,128)}, s32[8,2]{0,1:T(2,128)S(1)}, f32[8,1,3072]{2,1,0:T(1,128)S(1)}, s32[]{:T(128)}) while((s32[]{:T(128)}, f32[384,3797]{1,0:T(8,128)}, s32[8,2]{0,1:T(2,128)S(1)}, f32[8,1,3072]{2,1,0:T(1,128)S(1)}, s32[]{:T(128)}) %tuple.84), condition=%wide.while_cond.1, body=%wide.while_body.1.sunk | while | flops 2 | bytes 24685 | solution.py:28
  503.7 24.5 %while.19 = (s32[]{:T(128)}, bf16[384,4096]{1,0:T(8,128)(2,1)}, s32[8,2]{0,1:T(2,128)S(1)}, bf16[8,1,3456]{2,0,1:T(8,128)(2,1)S(1)}, s32[]{:T(128)}, /*index=5*/s32[]{:T(128)}) while((s32[]{:T(128)}, bf16[384,4096]{1,0:T(8,128)(2,1)}, s32[8,2]{0,1:T(2,128)S(1)}, bf16[8,1,3456]{2,0,1:T(8,128)(2,1)S(1)}, s32[]{:T(128)}, /*index=5*/s32[]{:T(128)}) %tuple.81), condition=%wide.while_cond, body=%wide.while_body.sunk | while | flops 2 | bytes 27765 | solution.py:27
  533.4 23.6 %while.20 = (s32[]{:T(128)}, f32[384,3797]{1,0:T(8,128)}, s32[8,2]{0,1:T(2,128)S(1)}, f32[8,1,3072]{2,1,0:T(1,128)S(1)}, s32[]{:T(128)}) while((s32[]{:T(128)}, f32[384,3797]{1,0:T(8,128)}, s32[8,2]{0,1:T(2,128)S(1)}, f32[8,1,3072]{2,1,0:T(1,128)S(1)}, s32[]{:T(128)}) %tuple.84), condition=%wide.while_cond.1, body=%wide.while_body.1.sunk | while | flops 2 | bytes 24685 | solution.py:28
  559.8 10.7 %all_to_all.5 = f32[8,1,3072]{2,1,0:T(1,128)S(1)} all-to-all(f32[8,1,3072]{2,1,0:T(1,128)S(1)} %reshape.180), channel_id=1, replica_groups=mesh['span'=2,'tmpl'=2,'stn'=8] {'stn'}, dimensions={0} | all-to-all | bytes 196608 | tf_op jit(solution)/shard_map/all_to_all | solution.py:93
  (681 shorter events, 464.8 us)
Async XLA Ops:
  6.5 3.0 copy-start
  6.5 50.0 %all-gather.2.cloned.1.call-start = ((), (), s32[]{:S(2)}) async-start(), calls=%async_computation.1 | async-start | bytes 4718592 | tf_op jit(solution)/shard_map/all_gather | solution.py:51
  73.1 2.7 copy-start.1
Sparse Core Ops, SparseCore 0:
  8.9 47.6 all-gather.1
where the time goes:
time: 586 us; the launch traced here: 578 us
  local copies, waits for them, and re-layouts  457 us (78%)
  waiting for transfers between devices  43.2 us (7%)
  other arithmetic  25.2 us (4%)
  loops' own time  20.5 us (3%)
  between operations  13.5 us (2%)
  blocking collectives  10.7 us (2%)
  matrix products  8.11 us (1%)
    gather x448, local copies, waits for them, and re-layouts  382 us
    all_gather x1, waiting for transfers between devices, shards(): series = lax.all_gather(signal, 'tmpl', axis=1, tiled=True)  42.4 us
    while x16, local copies, waits for them, and re-layouts  19.7 us
    another operation x1, loops' own time, shards(): stacks = lax.map(run_entry, jnp.arange(capacity, dtype=jnp.int32))  17.7 us
    another operation x16, local copies, waits for them, and re-layouts, toeplitz_tiles(): repeated = jnp.tile(padded, 128)[:128 * 640].reshape(128, 640)  12.1 us
  transfers between devices with their start and end apart: 1, of which 1 were waited for; matrix products, arithmetic and copies ran while one was open for 1% of the time, Pallas kernels for 0%

commit v1 on v0

v1 whole, which is shorter than its diff:
```python
import functools
import jax
import jax.numpy as jnp
from jax import lax
from jax.experimental import pallas as pl
from jax.experimental.pallas import tpu as pltpu
from jax.sharding import PartitionSpec as P

NT = 3072
LANES = 128
eps_value = 1e-05
KERNEL_VMEM = 24 << 20


def touch_of(groups_ref, k):
    station = lax.axis_index("stn")
    touch = jnp.int32(0)
    for g in range(1, groups_ref.shape[0]):
        touch = jnp.where(groups_ref[g, k] == station, g, touch)
    return touch


def toeplitz_kernel(slots, length, span, groups_ref, waves_ref, tiles_ref, inv_ref):
    half = jnp.zeros((slots, span - waves_ref.shape[3]), jnp.float32)

    def one_template(k, carry):
        touch = touch_of(groups_ref, k)
        waves = waves_ref[k, touch].astype(jnp.float32)
        power = jnp.sum(waves * waves, axis=1, keepdims=True) / length
        inv = 1.0 / (length * jnp.sqrt(power + eps_value))
        inv_ref[pl.ds(k * slots, slots), :] = jnp.broadcast_to(inv, (slots, LANES))
        padded = jnp.concatenate([waves, half], axis=1)
        for s in range(slots):
            row = jnp.broadcast_to(padded[s : s + 1, :], (LANES, span))
            rolled = pltpu.roll(row, 0, 1, stride=1, stride_axis=0)
            tiles_ref[k * slots + s] = rolled.astype(jnp.bfloat16)
        return carry

    lax.fori_loop(0, waves_ref.shape[0], one_template, 0)


def make_tiles(groups, waves):
    rows, _, slots, length = waves.shape
    span = LANES * (-(-(LANES + length - 1) // LANES))
    return pl.pallas_call(
        functools.partial(toeplitz_kernel, slots, length, span),
        out_shape=(
            jax.ShapeDtypeStruct((rows * slots, LANES, span), jnp.bfloat16),
            jax.ShapeDtypeStruct((rows * slots, LANES), jnp.float32),
        ),
        in_specs=[
            pl.BlockSpec(memory_space=pltpu.SMEM),
            pl.BlockSpec(memory_space=pltpu.VMEM),
        ],
        out_specs=(
            pl.BlockSpec(memory_space=pltpu.VMEM),
            pl.BlockSpec(memory_space=pltpu.VMEM),
        ),
        name="toeplitz",
        cost_estimate=pl.CostEstimate(flops=10000000, bytes_accessed=9000000, transcendentals=0),
        compiler_params=pltpu.CompilerParams(vmem_limit_bytes=KERNEL_VMEM),
    )(groups, waves)


def stack_kernel(slots, length, blocks, pieces, groups_ref, shift_ref, *refs):
    piece_refs, (tiles_ref, inv_ref, band_ref, out_ref, raw, rolled, aligned, sums) = refs[:pieces], refs[pieces:]
    rows = tiles_ref.shape[0]
    taps = tiles_ref.shape[2] // LANES
    pitch = raw.shape[0] // rows
    wide = aligned.shape[0] // slots
    raw[...] = jnp.zeros_like(raw)
    rolled[...] = jnp.zeros_like(rolled)
    for i, piece in enumerate(piece_refs):
        start = 0
        if pieces == 2:
            me = lax.axis_index("tmpl")
            start = (me if i == 0 else 1 - me) * (piece.shape[1] // LANES)
        for a in range(piece.shape[1] // LANES):
            for r in range(0, rows, 8):
                part = piece[r : r + 8, a * LANES : (a + 1) * LANES].astype(jnp.float32)
                raw[pl.ds(r * pitch + start + a, 8, stride=pitch), :] = part
    lane = lax.broadcasted_iota(jnp.int32, (wide, LANES), 1)

    def one_template(k, carry):
        touch = touch_of(groups_ref, k)
        for s in range(slots):
            shift = shift_ref[k, touch, s]
            whole = shift // LANES
            fine = shift - whole * LANES
            base = (k * slots + s) * pitch + whole
            turned = pltpu.roll(raw[pl.ds(base, wide), :], LANES - fine, 1)
            rolled[s, 0:wide, :] = turned
            value = jnp.where(lane < LANES - fine, turned, rolled[s, pl.ds(1, wide), :])
            aligned[s * wide : (s + 1) * wide, :] = value
        value = aligned[...]
        square = value * value
        high = square.astype(jnp.bfloat16)
        low = (square - high.astype(jnp.float32)).astype(jnp.bfloat16)
        sums[...] = jnp.dot(
            jnp.concatenate([high, low], axis=1), band_ref[...], preferred_element_type=jnp.float32
        )
        total = jnp.zeros((blocks, LANES), jnp.float32)
        for s in range(slots):
            row = k * slots + s
            window = jnp.concatenate(
                [aligned[pl.ds(s * wide + o, blocks), :] for o in range(taps)], axis=1
            ).astype(jnp.bfloat16)
            correl = lax.dot_general(
                window, tiles_ref[row], (((1,), (1,)), ((), ())), preferred_element_type=jnp.float32
            )
            energy = sums[pl.ds(s * wide, blocks), 0:LANES]
            for o in range(1, taps):
                energy = energy + sums[pl.ds(s * wide + o, blocks), o * LANES : (o + 1) * LANES]
            scale = lax.rsqrt(energy / length + eps_value) * inv_ref[pl.ds(row, 1), :]
            total = total + correl * scale
        out_ref[k] = total
        return carry

    lax.fori_loop(0, out_ref.shape[0], one_template, 0)


def make_stacks(groups, shifts, pieces, tiles, inv, band, templates, length, moveout_blocks):
    rows, _, span = tiles.shape
    slots = rows // templates
    blocks = NT // LANES
    wide = 8 * (-(-(blocks + span // LANES - 1) // 8))
    depth = sum(p.shape[1] for p in pieces) // LANES
    pitch = 8 * (-(-max(depth, wide + moveout_blocks) // 8))
    vmem = pl.BlockSpec(memory_space=pltpu.VMEM)
    smem = pl.BlockSpec(memory_space=pltpu.SMEM)
    return pl.pallas_call(
        functools.partial(stack_kernel, slots, length, blocks, len(pieces)),
        out_shape=jax.ShapeDtypeStruct((templates, blocks, LANES), jnp.float32),
        in_specs=[smem, smem] + [vmem] * (len(pieces) + 3),
        out_specs=vmem,
        scratch_shapes=[
            pltpu.VMEM((rows * pitch, LANES), jnp.float32),
            pltpu.VMEM((slots, wide + 8, LANES), jnp.float32),
            pltpu.VMEM((slots * wide, LANES), jnp.float32),
            pltpu.VMEM((slots * wide, span), jnp.float32),
        ],
        name="stack",
        cost_estimate=pl.CostEstimate(flops=400000000, bytes_accessed=9000000, transcendentals=0),
        compiler_params=pltpu.CompilerParams(vmem_limit_bytes=KERNEL_VMEM),
    )(groups, shifts, *pieces, tiles, inv, band)


def band_matrix(length, span):
    taps = span // LANES
    c = lax.broadcasted_iota(jnp.int32, (LANES, taps, LANES), 0)
    o = lax.broadcasted_iota(jnp.int32, (LANES, taps, LANES), 1)
    b = lax.broadcasted_iota(jnp.int32, (LANES, taps, LANES), 2)
    lag = LANES * o + c - b
    one = ((lag >= 0) & (lag < length)).astype(jnp.bfloat16).reshape(LANES, span)
    return jnp.concatenate([one, one], axis=0)


def pick_rows(groups, offsets, station, signal):
    count = signal.shape[0]
    here = (groups == station)[:, :, None, None]
    place = lax.broadcasted_iota(jnp.int32, (1, 1, 1, count), 3)
    hot = jnp.any(here & (offsets[..., None] == place), axis=1)
    hot = hot.reshape(-1, count).astype(signal.dtype)
    return jnp.dot(hot, signal, preferred_element_type=jnp.float32).astype(signal.dtype)


def sum_to_owner(stacks):
    stations = stacks.shape[0]
    if stations & (stations - 1):
        got = lax.all_to_all(stacks, "stn", split_axis=0, concat_axis=0, tiled=True)
        return jnp.sum(got, axis=0)
    me = lax.axis_index("stn")
    step = 1
    while step < stations:
        pairs = stacks.reshape((-1, 2) + stacks.shape[1:])
        bit = (me // step) % 2
        kept = lax.dynamic_index_in_dim(pairs, bit, 1, False)
        sent = lax.dynamic_index_in_dim(pairs, 1 - bit, 1, False)
        stacks = kept + lax.ppermute(sent, "stn", [(j, j ^ step) for j in range(stations)])
        step *= 2
    return stacks[0]


def shards(signal, waveforms, station_groups, channel_offsets, moveouts):
    templates, touches, slots, length = waveforms.shape
    count, samples = signal.shape
    parts = lax.axis_size("tmpl")
    stations = lax.axis_size("stn")
    station = lax.axis_index("stn")
    groups = station_groups.T
    if parts == 2:
        swap = [(0, 1), (1, 0)]
        asked = lax.ppermute(station_groups, "tmpl", swap), lax.ppermute(channel_offsets, "tmpl", swap)
        own = pick_rows(station_groups, channel_offsets, station, signal)
        sent = pick_rows(*asked, station, signal)
        sent, groups, own = lax.optimization_barrier((sent, groups, own))
        got = lax.ppermute(sent, "tmpl", swap)
        pieces = (own, got)
    else:
        asked = [lax.all_gather(x, "tmpl", axis=0, tiled=True) for x in (station_groups, channel_offsets)]
        sent = pick_rows(*asked, station, signal).reshape(parts, templates * slots, samples)
        got = lax.all_to_all(sent, "tmpl", split_axis=0, concat_axis=0, tiled=True)
        pieces = (got.transpose(1, 0, 2).reshape(templates * slots, parts * samples),)
    tiles, inv = make_tiles(groups, waveforms)
    band = band_matrix(length, tiles.shape[2])
    moveout_blocks = (parts * samples - NT - length) // LANES
    stacks = make_stacks(groups, moveouts, pieces, tiles, inv, band, templates, length, moveout_blocks)
    own_rows = templates // stations
    total = sum_to_owner(stacks.reshape((stations, own_rows) + stacks.shape[1:]))
    return total.reshape(own_rows, NT)


def solution(mesh):
    in_specs = (
        P("stn", ("span", "tmpl")),
        P("tmpl", None, None, None),
        P("tmpl", None),
        P("tmpl", None, None),
        P("tmpl", None, None),
    )
    out_specs = P(("tmpl", "stn"), "span")
    return jax.shard_map(shards, mesh=mesh, in_specs=in_specs, out_specs=out_specs, check_vma=False)
```

time: 586 us -> 31.1 us (0.05); the launches traced: 578 us -> 30.8 us
  local copies, waits for them, and re-layouts: 457 us -> 0.31 us
  waiting for transfers between devices: 43.2 us -> 8.84 us
  other arithmetic: 25.2 us -> 2.43 us
  loops' own time: 20.5 us -> 0 us
  between operations: 13.5 us -> 0.18 us
  blocking collectives: 10.7 us -> 0 us
  Pallas kernels: 0 us -> 9.75 us
  starting transfers between devices: 0.01 us -> 8.53 us
  matrix products: 8.11 us -> 0.79 us
    gather x452 -> x0, local copies, waits for them, and re-layouts: 386 us -> none
    all_gather x1 -> x0, waiting for transfers between devices: 42.4 us -> none  [shards(): series = lax.all_gather(signal, 'tmpl', axis=1, tiled=True)]
    while x17 -> x0, local copies, waits for them, and re-layouts: 26.2 us -> none
    another operation x36 -> x0, local copies, waits for them, and re-layouts: 22.5 us -> none  [the longest x16 12.1 us: toeplitz_tiles(): repeated = jnp.tile(padded, 128)[:128 * 640].reshape(128, 640)]
    another operation x17 -> x0, loops' own time: 20.5 us -> none  [the longest x1 17.7 us: shards(): stacks = lax.map(run_entry, jnp.arange(capacity, dtype=jnp.int32))]
    all_to_all x1 -> x0, blocking collectives: 10.7 us -> none  [shards(): lax.all_to_all(by_owner, 'stn', split_axis=0, concat_axis=0, tiled=True)]
    dynamic_slice x16 -> x0, local copies, waits for them, and re-layouts: 10.7 us -> none  [the longest x8 5.36 us: run_entry(): return jnp.where(is_live[entry_num], stacked, 0.0)]
    pallas_call x0 -> x2, Pallas kernels: none -> 9.75 us  [the longest x1 6.23 us: make_stacks(): pl.pallas_call(functools.partial(stack_kernel, slots, length, blocks, len...]
  transfers between devices with their start and end apart: 1 -> 6, of which waited for: 1 -> 5; matrix products, arithmetic and copies ran while one was open for 1% -> 8% of each run, Pallas kernels for 0% -> 11%
where the time goes in v1:
time: 31.1 us; the launch traced here: 30.8 us
  Pallas kernels  9.75 us (31%)
  waiting for transfers between devices  8.84 us (28%)
  starting transfers between devices  8.53 us (27%)
  other arithmetic  2.43 us (8%)
  matrix products  0.79 us (3%)
    pallas_call x1, Pallas kernels, make_stacks(): pl.pallas_call(functools.partial(stack_kernel, slots, length, blocks, len...  6.23 us
    ppermute x3, starting transfers between devices, sum_to_owner(): lax.ppermute(sent, 'stn', [(j, j ^ step) for j in range(stations)])  4.98 us
    ppermute x3, waiting for transfers between devices, sum_to_owner(): lax.ppermute(sent, 'stn', [(j, j ^ step) for j in range(stations)])  4.81 us
    pallas_call x1, Pallas kernels, make_tiles(): pl.pallas_call(functools.partial(toeplitz_kernel, slots, length, span), o...  3.53 us
    ppermute x1, starting transfers between devices, shards(): lax.ppermute(channel_offsets, 'tmpl', swap)  2.97 us
    ppermute x1, waiting for transfers between devices, shards(): got = lax.ppermute(sent, 'tmpl', swap)  2.51 us
    ppermute x1, waiting for transfers between devices, shards(): lax.ppermute(station_groups, 'tmpl', swap)  1.52 us
    reduce_or x2, other arithmetic, pick_rows(): hot = jnp.any(here & (offsets[..., None] == place), axis=1)  1 us
  transfers between devices with their start and end apart: 6, of which 5 were waited for; matrix products, arithmetic and copies ran while one was open for 8% of the time, Pallas kernels for 11%

profile of v1, /device:TPU:0, one launch (start us, length us, event | category | flops | bytes accessed | tf_op | source)
XLA Modules:
  0.0 30.8 jit_solution(17803275719365271293)
XLA Ops:
  0.0 3.0 %collective-permute-start.1 = (s32[8,4,8]{2,1,0:T(4,128)}, s32[8,4,8]{2,1,0:T(4,128)S(1)}, u32[]{:S(2)}, u32[]{:S(2)}) collective-permute-start(s32[8,4,8]{2,1,0:T(4,128)} %param.8), channel_id=1, source_target_pairs={{0,8},{8,0},{1,9},{9,1},{2,10},{10,2},{3,11},{11,3},{4,12},{12,4},... | collective-permute-start | bytes 3080 | tf_op jit(solution)/shard_map/ppermute | solution.py:193
  3.0 0.1 collective-permute-start
  3.0 0.7 %broadcast_compare_fusion = pred[8,4]{0,1:T(4,128)(4,1)S(1)} fusion(s32[8,4]{0,1:T(4,128)} %param.7, s32[]{:T(128)S(6)} %axis_index.16), kind=kLoop, calls=%fused_computation.23 | loop fusion | flops 32 | bytes 164 | tf_op jit(solution)/shard_map/eq | solution.py:160
  3.8 0.1 copy.11
  3.9 0.9 %fusion.3 = pred[8,8,384]{2,1,0:T(8,128)(4,1)S(1)} fusion(s32[8,4,8]{2,1,0:T(4,128)} %param.8, pred[8,4]{1,0:T(8,128)(4,1)S(1)} %copy.11), kind=kLoop, calls=%fused_computation.8 | loop fusion | flops 270336 | bytes 25632 | tf_op jit(solution)/shard_map/reduce_or | solution.py:162
  4.7 0.1 iota_bitcast_fusion
  4.8 0.4 %convolution_convert_fusion.refs_0_ = bf16[64,2048]{1,0:T(8,128)(2,1)S(1)} fusion(bf16[384,2048]{1,0:T(8,128)(2,1)S(1)} %copy-done, pred[8,8,384]{2,1,0:T(8,128)(4,1)S(1)} %fusion.3), kind=kOutput, calls=%fused_computation | convolution fusion | flops 100794368 | bytes 1859584 | tf_op jit(solution)/shard_map/dot_general | solution.py:164
  5.2 0.0 copy-start.3
  5.2 1.5 %collective-permute-done = s32[8,4]{0,1:T(4,128)S(1)} collective-permute-done((s32[8,4]{0,1:T(4,128)}, s32[8,4]{0,1:T(4,128)S(1)}, u32[]{:S(2)}, u32[]{:S(2)}) %collective-permute-start) | collective-permute-done | bytes 160 | tf_op jit(solution)/shard_map/ppermute | solution.py:193
  6.8 0.1 copy.10
  6.9 0.1 fusion.1
  7.0 0.4 %convolution_convert_fusion.1 = bf16[64,2048]{1,0:T(8,128)(2,1)S(1)} fusion(bf16[384,2048]{1,0:T(8,128)(2,1)S(1)} %copy-done, pred[8,8,384]{2,1,0:T(8,128)(4,1)S(1)} %fusion.1), kind=kOutput, calls=%fused_computation.1 | convolution fusion | flops 100794368 | bytes 1859584 | tf_op jit(solution)/shard_map/dot_general | solution.py:164
  7.4 0.5 %collective-permute-start.2 = (bf16[64,2048]{1,0:T(8,128)(2,1)S(1)}, bf16[64,2048]{1,0:T(8,128)(2,1)S(1)}, u32[]{:S(2)}, u32[]{:S(2)}) collective-permute-start(bf16[64,2048]{1,0:T(8,128)(2,1)S(1)} %convolution_convert_fusion.1), channel_id=1, source_target_pairs={{0,8},{8,0},{1,9},{9,1},{2,10},{10,2},{3,11},{11,3},{4,12},{12,4},... | collective-permute-start | bytes 786440 | tf_op jit(solution)/shard_map/ppermute | solution.py:197
  7.9 0.1 fusion.6
  8.1 3.5 %toeplitz.1 = (bf16[64,128,512]{2,1,0:T(8,128)(2,1)S(1)}, f32[64,128]{1,0:T(8,128)S(1)}) custom-call(s32[4,8]{1,0:T(4,128)S(1)} %bitcast.26, bf16[8,4,8,300]{3,2,1,0:T(8,128)(2,1)S(1)} %copy-done.1), custom_call_target="tpu_custom_call" | custom-call | flops 10000000 | bytes 9000000 | tf_op jit(solution)/shard_map/toeplitz/pallas_call | solution.py:45
  11.6 2.5 %collective-permute-done.2.refs_1_ = bf16[64,2048]{1,0:T(8,128)(2,1)S(1)} collective-permute-done((bf16[64,2048]{1,0:T(8,128)(2,1)S(1)}, bf16[64,2048]{1,0:T(8,128)(2,1)S(1)}, u32[]{:S(2)}, u32[]{:S(2)}) %collective-permute-start.2) | collective-permute-done | bytes 262176 | tf_op jit(solution)/shard_map/ppermute | solution.py:197
  14.1 6.2 %stack.1 = f32[8,24,128]{2,1,0:T(8,128)S(1)} custom-call(s32[4,8]{1,0:T(4,128)S(1)} %bitcast.27, s32[8,4,8]{2,1,0:T(4,128)S(1)} %copy-done.3, bf16[64,2048]{1,0:T(8,128)(2,1)S(1)} %convolution_convert_fusion.refs_0_, bf16[64,2048]{1,0:T(8,128)(2,1)S(1)} %collective-permute-done.2.refs_1_, bf16[64,128,512]{2,1,0:T(8,128)(2,1)S(1)} %get-tuple-element.13.refs_2_, ...), custom_call_target="tpu_custom_call" | custom-call | flops 400000000 | bytes 9000000 | tf_op jit(solution)/shard_map/stack/pallas_call | solution.py:131
  20.4 0.1 collective-permute-start.3
  20.5 1.2 %collective-permute-done.3 = f32[4,1,24,128]{3,2,0,1:T(8,128)S(1)} collective-permute-done((f32[4,1,24,128]{3,2,0,1:T(8,128)S(1)}, f32[4,1,24,128]{3,2,0,1:T(8,128)S(1)}, u32[]{:S(2)}, u32[]{:S(2)}) %collective-permute-start.3) | collective-permute-done | bytes 49184 | tf_op jit(solution)/shard_map/ppermute | solution.py:179
  21.7 1.9 %collective-permute-start.4 = (f32[2,1,24,128]{3,2,1,0:T(8,128)S(1)}, f32[2,1,24,128]{3,2,1,0:T(8,128)S(1)}, u32[]{:S(2)}, u32[]{:S(2)}) collective-permute-start(f32[2,1,24,128]{3,2,1,0:T(8,128)S(1)} %dynamic-slice_bitcast_fusion.1), channel_id=1, source_target_pairs={{0,2},{1,3},{2,0},{3,1},{4,6},{5,7},{6,4},{7,5},{8,10},{9,11},{10,... | collective-permute-start | bytes 73736 | tf_op jit(solution)/shard_map/ppermute | solution.py:179
  23.6 1.9 %collective-permute-done.4 = f32[2,1,24,128]{3,2,1,0:T(8,128)S(1)} collective-permute-done((f32[2,1,24,128]{3,2,1,0:T(8,128)S(1)}, f32[2,1,24,128]{3,2,1,0:T(8,128)S(1)}, u32[]{:S(2)}, u32[]{:S(2)}) %collective-permute-start.4) | collective-permute-done | bytes 24608 | tf_op jit(solution)/shard_map/ppermute | solution.py:179
  25.6 3.0 %collective-permute-start.5 = (f32[1,1,24,128]{3,2,1,0:T(8,128)S(1)}, f32[1,1,24,128]{3,2,1,0:T(8,128)S(1)}, u32[]{:S(2)}, u32[]{:S(2)}) collective-permute-start(f32[1,1,24,128]{3,2,1,0:T(8,128)S(1)} %constant_dynamic-slice_fusion), channel_id=1, source_target_pairs={{0,4},{1,5},{2,6},{3,7},{4,0},{5,1},{6,2},{7,3},{8,12},{9,13},{10,... | collective-permute-start | bytes 36872 | tf_op jit(solution)/shard_map/ppermute | solution.py:179
  28.5 1.7 %collective-permute-done.5 = f32[1,1,24,128]{3,2,1,0:T(8,128)S(1)} collective-permute-done((f32[1,1,24,128]{3,2,1,0:T(8,128)S(1)}, f32[1,1,24,128]{3,2,1,0:T(8,128)S(1)}, u32[]{:S(2)}, u32[]{:S(2)}) %collective-permute-start.5) | collective-permute-done | bytes 12320 | tf_op jit(solution)/shard_map/ppermute | solution.py:179
  30.2 0.6 %dynamic-slice_add_fusion = f32[1,1,24,128]{3,2,1,0:T(8,128)} fusion(f32[1,1,24,128]{3,2,1,0:T(8,128)S(1)} %collective-permute-done.5, f32[2,1,24,128]{3,2,1,0:T(8,128)S(1)} %bitcast_add_fusion.1, s32[]{:T(128)S(6)} %select_n.53), kind=kLoop, calls=%fused_computation.19 | loop fusion | flops 3072 | bytes 36868 | tf_op jit(solution)/shard_map/add | solution.py:179
  (16 shorter events, 0.1 us)
Async XLA Ops:
  0.0 4.8 %copy-start = (bf16[384,2048]{1,0:T(8,128)(2,1)S(1)}, bf16[384,2048]{1,0:T(8,128)(2,1)}, u32[]{:S(2)}) copy-start(bf16[384,2048]{1,0:T(8,128)(2,1)} %param.5) | copy-start | bytes 4718596
  0.0 6.9 %collective-permute-start.1 = (s32[8,4,8]{2,1,0:T(4,128)}, s32[8,4,8]{2,1,0:T(4,128)S(1)}, u32[]{:S(2)}, u32[]{:S(2)}) collective-permute-start(s32[8,4,8]{2,1,0:T(4,128)} %param.8), channel_id=1, source_target_pairs={{0,8},{8,0},{1,9},{9,1},{2,10},{10,2},{3,11},{11,3},{4,12},{12,4},... | collective-permute-start | bytes 3080 | tf_op jit(solution)/shard_map/ppermute | solution.py:193
  3.0 3.8 %collective-permute-start = (s32[8,4]{0,1:T(4,128)}, s32[8,4]{0,1:T(4,128)S(1)}, u32[]{:S(2)}, u32[]{:S(2)}) collective-permute-start(s32[8,4]{0,1:T(4,128)} %param.7), channel_id=1, source_target_pairs={{0,8},{8,0},{1,9},{9,1},{2,10},{10,2},{3,11},{11,3},{4,12},{12,4},... | collective-permute-start | bytes 392 | tf_op jit(solution)/shard_map/ppermute | solution.py:193
  5.2 2.9 %copy-start.1 = (bf16[8,4,8,300]{3,2,1,0:T(8,128)(2,1)S(1)}, bf16[8,4,8,300]{3,2,1,0:T(8,128)(2,1)}, u32[]{:S(2)}) copy-start(bf16[8,4,8,300]{3,2,1,0:T(8,128)(2,1)} %waves_ref.1) | copy-start | bytes 460804
  5.2 2.8 %copy-start.2 = (s32[8,4]{0,1:T(4,128)S(1)}, s32[8,4]{0,1:T(4,128)}, u32[]{:S(2)}) copy-start(s32[8,4]{0,1:T(4,128)} %param.7) | copy-start | bytes 388
  5.2 8.9 %copy-start.3 = (s32[8,4,8]{2,1,0:T(4,128)S(1)}, s32[8,4,8]{2,1,0:T(4,128)}, u32[]{:S(2)}) copy-start(s32[8,4,8]{2,1,0:T(4,128)} %shift_ref.1) | copy-start | bytes 3076
  7.4 6.7 %collective-permute-start.2 = (bf16[64,2048]{1,0:T(8,128)(2,1)S(1)}, bf16[64,2048]{1,0:T(8,128)(2,1)S(1)}, u32[]{:S(2)}, u32[]{:S(2)}) collective-permute-start(bf16[64,2048]{1,0:T(8,128)(2,1)S(1)} %convolution_convert_fusion.1), channel_id=1, source_target_pairs={{0,8},{8,0},{1,9},{9,1},{2,10},{10,2},{3,11},{11,3},{4,12},{12,4},... | collective-permute-start | bytes 786440 | tf_op jit(solution)/shard_map/ppermute | solution.py:197
  20.4 1.3 %collective-permute-start.3 = (f32[4,1,24,128]{3,2,0,1:T(8,128)S(1)}, f32[4,1,24,128]{3,2,0,1:T(8,128)S(1)}, u32[]{:S(2)}, u32[]{:S(2)}) collective-permute-start(f32[4,1,24,128]{3,2,0,1:T(8,128)S(1)} %dynamic-slice_bitcast_fusion), channel_id=1, source_target_pairs={{0,1},{1,0},{2,3},{3,2},{4,5},{5,4},{6,7},{7,6},{8,9},{9,8},{10,11... | collective-permute-start | bytes 147464 | tf_op jit(solution)/shard_map/ppermute | solution.py:179
  21.7 3.9 %collective-permute-start.4 = (f32[2,1,24,128]{3,2,1,0:T(8,128)S(1)}, f32[2,1,24,128]{3,2,1,0:T(8,128)S(1)}, u32[]{:S(2)}, u32[]{:S(2)}) collective-permute-start(f32[2,1,24,128]{3,2,1,0:T(8,128)S(1)} %dynamic-slice_bitcast_fusion.1), channel_id=1, source_target_pairs={{0,2},{1,3},{2,0},{3,1},{4,6},{5,7},{6,4},{7,5},{8,10},{9,11},{10,... | collective-permute-start | bytes 73736 | tf_op jit(solution)/shard_map/ppermute | solution.py:179
  25.6 4.7 %collective-permute-start.5 = (f32[1,1,24,128]{3,2,1,0:T(8,128)S(1)}, f32[1,1,24,128]{3,2,1,0:T(8,128)S(1)}, u32[]{:S(2)}, u32[]{:S(2)}) collective-permute-start(f32[1,1,24,128]{3,2,1,0:T(8,128)S(1)} %constant_dynamic-slice_fusion), channel_id=1, source_target_pairs={{0,4},{1,5},{2,6},{3,7},{4,0},{5,1},{6,2},{7,3},{8,12},{9,13},{10,... | collective-permute-start | bytes 36872 | tf_op jit(solution)/shard_map/ppermute | solution.py:179

commit v2 on v1

v2 whole, which is shorter than its diff:
```python
import functools
import jax
import jax.numpy as jnp
from jax import lax
from jax.experimental import pallas as pl
from jax.experimental.pallas import tpu as pltpu
from jax.sharding import PartitionSpec as P

NT = 3072
LANES = 128
eps_value = 1e-05
KERNEL_VMEM = 24 << 20


def order_of(stations):
    bits = stations.bit_length() - 1
    reverse = lambda m: sum(((m >> b) & 1) << (bits - 1 - b) for b in range(bits))
    return sorted(range(stations), key=reverse, reverse=True)


def template_at(position, stations, templates, station):
    own_rows = templates // stations
    entry = order_of(stations)[position // own_rows]
    return (entry ^ station) * own_rows + position % own_rows


def touch_of(groups_ref, k, station):
    touch = jnp.int32(0)
    for g in range(1, groups_ref.shape[0]):
        touch = jnp.where(groups_ref[g, k] == station, g, touch)
    return touch


def toeplitz_kernel(slots, length, span, stations, groups_ref, waves_ref, tiles_ref, inv_ref):
    templates = waves_ref.shape[0]
    station = lax.axis_index("stn")
    tail = jnp.zeros((slots, span - length), jnp.float32)
    for p in range(templates):
        k = template_at(p, stations, templates, station)
        waves = waves_ref[k, touch_of(groups_ref, k, station)].astype(jnp.float32)
        power = jnp.sum(waves * waves, axis=1, keepdims=True) / length
        inv = 1.0 / (length * jnp.sqrt(power + eps_value))
        inv_ref[p * slots : (p + 1) * slots, :] = jnp.broadcast_to(inv, (slots, LANES))
        padded = jnp.concatenate([waves, tail], axis=1)
        for s in range(slots):
            row = jnp.broadcast_to(padded[s : s + 1, :], (LANES, span))
            rolled = pltpu.roll(row, 0, 1, stride=1, stride_axis=0)
            tiles_ref[p * slots + s] = rolled.astype(jnp.bfloat16)


def make_tiles(groups, waves, stations):
    templates, _, slots, length = waves.shape
    span = LANES * (-(-(LANES + length - 1) // LANES))
    vmem = pl.BlockSpec(memory_space=pltpu.VMEM)
    return pl.pallas_call(
        functools.partial(toeplitz_kernel, slots, length, span, stations),
        out_shape=(
            jax.ShapeDtypeStruct((templates * slots, LANES, span), jnp.bfloat16),
            jax.ShapeDtypeStruct((templates * slots, LANES), jnp.float32),
        ),
        in_specs=[pl.BlockSpec(memory_space=pltpu.SMEM), vmem],
        out_specs=(vmem, vmem),
        name="toeplitz",
        cost_estimate=pl.CostEstimate(flops=10000000, bytes_accessed=9000000, transcendentals=0),
        compiler_params=pltpu.CompilerParams(vmem_limit_bytes=KERNEL_VMEM),
    )(groups, waves)


def stack_kernel(slots, length, blocks, stations, positions, starts, groups_ref, shift_ref, *refs):
    pieces = len(starts)
    piece_refs, (tiles_ref, inv_ref, band_ref, out_ref, raw, rolled, aligned, sums) = refs[:pieces], refs[pieces:]
    templates = tiles_ref.shape[0] // slots
    taps = tiles_ref.shape[2] // LANES
    rows = len(positions) * slots
    pitch = raw.shape[0] // rows
    wide = aligned.shape[0] // rows
    station = lax.axis_index("stn")
    for i, piece in enumerate(piece_refs):
        start = 0
        if pieces == 2:
            me = lax.axis_index("tmpl")
            start = (me if i == 0 else 1 - me) * (piece.shape[1] // LANES)
        for a in range(piece.shape[1] // LANES):
            for r in range(0, rows, 8):
                first = starts[i] + r
                part = piece[first : first + 8, a * LANES : (a + 1) * LANES].astype(jnp.float32)
                raw[pl.ds(r * pitch + start + a, 8, stride=pitch), :] = part
    lane = lax.broadcasted_iota(jnp.int32, (wide, LANES), 1)

    def align(i):
        k = template_at(positions[i], stations, templates, station)
        touch = touch_of(groups_ref, k, station)
        for s in range(slots):
            row = i * slots + s
            shift = shift_ref[k, touch, s]
            whole = shift >> 7
            fine = shift & (LANES - 1)
            turned = pltpu.roll(raw[pl.ds(row * pitch + whole, wide), :], LANES - fine, 1)
            rolled[row, 0:wide, :] = turned
            value = jnp.where(lane < LANES - fine, turned, rolled[row, pl.ds(1, wide), :])
            aligned[row * wide : (row + 1) * wide, :] = value
        span = pl.ds(i * slots * wide, slots * wide)
        value = aligned[span, :]
        square = value * value
        high = square.astype(jnp.bfloat16)
        low = (square - high.astype(jnp.float32)).astype(jnp.bfloat16)
        sums[span, :] = jnp.dot(
            jnp.concatenate([high, low], axis=1), band_ref[...], preferred_element_type=jnp.float32
        )

    def stack(i):
        total = jnp.zeros((blocks, LANES), jnp.float32)
        for s in range(slots):
            row = positions[i] * slots + s
            first = (i * slots + s) * wide
            window = jnp.concatenate(
                [aligned[pl.ds(first + o, blocks), :] for o in range(taps)], axis=1
            ).astype(jnp.bfloat16)
            correl = lax.dot_general(
                window, tiles_ref[row], (((1,), (1,)), ((), ())), preferred_element_type=jnp.float32
            )
            energy = sums[pl.ds(first, blocks), 0:LANES]
            for o in range(1, taps):
                energy = energy + sums[pl.ds(first + o, blocks), o * LANES : (o + 1) * LANES]
            scale = lax.rsqrt(energy / length + eps_value) * inv_ref[pl.ds(row, 1), :]
            total = total + correl * scale
        out_ref[i] = total

    for i in range(len(positions)):
        align(i)
        if i:
            stack(i - 1)
    stack(len(positions) - 1)


def make_stacks(positions, groups, shifts, pieces, tiles, inv, band, length, stations):
    templates, _, slots = shifts.shape
    span = tiles.shape[2]
    rows = len(positions) * slots
    blocks = NT // LANES
    wide = 8 * (-(-(blocks + span // LANES - 1) // 8))
    depth = sum(p.shape[1] for p, _ in pieces) // LANES
    pitch = 8 * (-(-(depth + wide - blocks) // 8))
    vmem = pl.BlockSpec(memory_space=pltpu.VMEM)
    smem = pl.BlockSpec(memory_space=pltpu.SMEM)
    return pl.pallas_call(
        functools.partial(
            stack_kernel, slots, length, blocks, stations, positions, tuple(first for _, first in pieces)
        ),
        out_shape=jax.ShapeDtypeStruct((len(positions), blocks, LANES), jnp.float32),
        in_specs=[smem, smem] + [vmem] * (len(pieces) + 3),
        out_specs=vmem,
        scratch_shapes=[
            pltpu.VMEM((rows * pitch, LANES), jnp.float32),
            pltpu.VMEM((rows, wide + 8, LANES), jnp.float32),
            pltpu.VMEM((rows * wide, LANES), jnp.float32),
            pltpu.VMEM((rows * wide, span), jnp.float32),
        ],
        name="stack",
        cost_estimate=pl.CostEstimate(
            flops=50000000 * len(positions), bytes_accessed=1000000 * len(positions), transcendentals=0
        ),
        compiler_params=pltpu.CompilerParams(vmem_limit_bytes=KERNEL_VMEM),
    )(groups, shifts, *[p for p, _ in pieces], tiles, inv, band)


def band_matrix(length, span):
    taps = span // LANES
    c = lax.broadcasted_iota(jnp.int32, (LANES, taps, LANES), 0)
    o = lax.broadcasted_iota(jnp.int32, (LANES, taps, LANES), 1)
    b = lax.broadcasted_iota(jnp.int32, (LANES, taps, LANES), 2)
    lag = LANES * o + c - b
    one = ((lag >= 0) & (lag < length)).astype(jnp.bfloat16).reshape(LANES, span)
    return jnp.concatenate([one, one], axis=0)


def pick_rows(groups, offsets, station, stations, signal):
    templates, _, slots = offsets.shape
    count = signal.shape[0]
    named = jnp.stack([template_at(p, stations, templates, station) for p in range(templates)])
    here = (groups == station)[None] & (lax.iota(jnp.int32, templates)[None] == named[:, None])[:, :, None]
    wanted = jnp.sum(jnp.where(here[..., None], offsets[None] + 1, 0), axis=(1, 2)) - 1
    hot = wanted[..., None] == lax.broadcasted_iota(jnp.int32, (1, 1, count), 2)
    hot = hot.reshape(templates * slots, count).astype(signal.dtype)
    return jnp.dot(hot, signal, preferred_element_type=jnp.float32).astype(signal.dtype)


def shards(signal, waveforms, station_groups, channel_offsets, moveouts):
    templates, touches, slots, length = waveforms.shape
    samples = signal.shape[1]
    parts = lax.axis_size("tmpl")
    stations = lax.axis_size("stn")
    station = lax.axis_index("stn")
    groups = station_groups.T
    half, quarter = templates // 2, templates // 4
    if parts == 2:
        swap = [(0, 1), (1, 0)]
        if templates == slots:
            packed = lax.optimization_barrier(jnp.concatenate([channel_offsets, groups[None]], axis=0))
            named, asked = [(x[templates].T, x[:templates]) for x in (packed, lax.ppermute(packed, "tmpl", swap))]
        else:
            named = station_groups, channel_offsets
            asked = [lax.ppermute(x, "tmpl", swap) for x in named]
        own = pick_rows(*named, station, stations, signal)
        asked, own = lax.optimization_barrier((asked, own))
        sent = pick_rows(*asked, station, stations, signal)
        sent = sent[: half * slots], sent[half * slots :]
        sent, groups = lax.optimization_barrier((sent, groups))
        early = lax.ppermute(sent[0], "tmpl", swap)

        def pieces(first):
            return (own, first * slots), (got[first >= half], first % half * slots)
    else:
        asked = [lax.all_gather(x, "tmpl", axis=0) for x in (station_groups, channel_offsets)]
        sent = jnp.stack([pick_rows(asked[0][i], asked[1][i], station, stations, signal) for i in range(parts)])
        got = lax.all_to_all(sent, "tmpl", split_axis=0, concat_axis=0, tiled=True)
        got = got.transpose(1, 0, 2).reshape(templates * slots, parts * samples)

        def pieces(first):
            return ((got, first * slots),)

    tiles, inv = make_tiles(groups, waveforms, stations)
    if parts == 2:
        late, inv = lax.optimization_barrier((sent[1], inv))
        got = early, lax.ppermute(late, "tmpl", swap)
    band = band_matrix(length, tiles.shape[2])

    def stacks(first, last):
        positions = tuple(range(first, last))
        return make_stacks(positions, groups, moveouts, pieces(first), tiles, inv, band, length, stations)

    def across(x, step):
        return lax.ppermute(x, "stn", [(j, j ^ step) for j in range(stations)])

    came = across(stacks(0, half), 1)
    left = stacks(half, half + quarter) + came[:quarter]
    came_left = across(left, 2)
    total = stacks(half + quarter, templates) + came[quarter:] + came_left
    step = 4
    while step < stations:
        middle = total.shape[0] // 2
        total = total[middle:] + across(total[:middle], step)
        step *= 2
    return total.reshape(templates // stations, NT)


def solution(mesh):
    in_specs = (
        P("stn", ("span", "tmpl")),
        P("tmpl", None, None, None),
        P("tmpl", None),
        P("tmpl", None, None),
        P("tmpl", None, None),
    )
    out_specs = P(("tmpl", "stn"), "span")
    return jax.shard_map(shards, mesh=mesh, in_specs=in_specs, out_specs=out_specs, check_vma=False)
```

time: 31.1 us -> 27.4 us (0.88)
  waiting for transfers between devices: 8.84 us -> 5.06 us
  starting transfers between devices: 8.53 us -> 9.47 us
  other arithmetic: 2.43 us -> 1.92 us
  Pallas kernels: 9.75 us -> 9.27 us
    ppermute x6, waiting for transfers between devices: 8.84 us -> 5.06 us  [the longest x3 2.32 us: across(): return lax.ppermute(x, 'stn', [(j, j ^ step) for j in range(stations)])]
    reduce_or x2 -> x0, other arithmetic: 1 us -> none  [pick_rows(): hot = jnp.any(here & (offsets[..., None] == place), axis=1)]
    ppermute x6, starting transfers between devices: 8.53 us -> 9.47 us  [the longest x3 4.33 us: across(): return lax.ppermute(x, 'stn', [(j, j ^ step) for j in range(stations)])]
    concatenate x0 -> x1, other arithmetic: none -> 0.86 us  [shards(): jnp.concatenate([channel_offsets, groups[None]], axis=0)]
    eq x2 -> x3, other arithmetic: 0.72 us -> 0.09 us  [the longest x1 0.08 us: pick_rows(): lax.iota(jnp.int32, templates)[None] == named[:, None]]
    pallas_call x2 -> x4, Pallas kernels: 9.75 us -> 9.27 us  [the longest x3 6.8 us: make_stacks(): pl.pallas_call(functools.partial(stack_kernel, slots, length, blocks, sta...]
    add x3 -> x5, other arithmetic: 0.61 us -> 0.63 us  [the longest x1 0.6 us: shards(): total = total[middle:] + across(total[:middle], step)]
  transfers between devices with their start and end apart: 6 -> 6, of which waited for: 5 -> 5; matrix products, arithmetic and copies ran while one was open for 8% -> 4% of each run, Pallas kernels for 11% -> 34%
where the time goes in v2:
time: 27.4 us; the launch traced here: 27.1 us
  starting transfers between devices  9.47 us (35%)
  Pallas kernels  9.27 us (34%)
  waiting for transfers between devices  5.06 us (18%)
  other arithmetic  1.92 us (7%)
  matrix products  0.87 us (3%)
  local copies, waits for them, and re-layouts  0.37 us (1%)
    pallas_call x3, Pallas kernels, make_stacks(): pl.pallas_call(functools.partial(stack_kernel, slots, length, blocks, sta...  6.8 us
    ppermute x3, starting transfers between devices, across(): return lax.ppermute(x, 'stn', [(j, j ^ step) for j in range(stations)])  4.33 us
    ppermute x1, starting transfers between devices, shards(): lax.ppermute(packed, 'tmpl', swap)  2.97 us
    pallas_call x1, Pallas kernels, make_tiles(): pl.pallas_call(functools.partial(toeplitz_kernel, slots, length, span, st...  2.46 us
    ppermute x3, waiting for transfers between devices, across(): return lax.ppermute(x, 'stn', [(j, j ^ step) for j in range(stations)])  2.32 us
    ppermute x1, starting transfers between devices, shards(): early = lax.ppermute(sent[0], 'tmpl', swap)  2.09 us
    ppermute x1, waiting for transfers between devices, shards(): got = (early, lax.ppermute(late, 'tmpl', swap))  1.11 us
    dot_general x2, matrix products, pick_rows(): jnp.dot(hot, signal, preferred_element_type=jnp.float32)  0.87 us
  transfers between devices with their start and end apart: 6, of which 5 were waited for; matrix products, arithmetic and copies ran while one was open for 4% of the time, Pallas kernels for 34%

profile of v2, /device:TPU:0, one launch (start us, length us, event | category | flops | bytes accessed | tf_op | source)
XLA Modules:
  0.0 27.1 jit_solution(5012344056115831345)
XLA Ops:
  0.0 0.9 %pad_add_fusion = s32[9,4,8]{2,1,0:T(4,128)S(1)} fusion(s32[1,4,8]{2,1,0:T(4,128)} %bitcast.26, s32[8,4,8]{2,1,0:T(4,128)} %param.8), kind=kLoop, calls=%fused_computation.16 | loop fusion | flops 288 | bytes 2304 | tf_op jit(solution)/shard_map/concatenate | solution.py:199
  0.9 3.0 %collective-permute-start = (s32[9,4,8]{2,1,0:T(4,128)S(1)}, s32[9,4,8]{2,1,0:T(4,128)S(1)}, u32[]{:S(2)}, u32[]{:S(2)}) collective-permute-start(s32[9,4,8]{2,1,0:T(4,128)S(1)} %pad_add_fusion), channel_id=1, source_target_pairs={{0,8},{8,0},{1,9},{9,1},{2,10},{10,2},{3,11},{11,3},{4,12},{12,4},... | collective-permute-start | bytes 3464 | tf_op jit(solution)/shard_map/ppermute | solution.py:200
  3.9 0.1 stack.47
  3.9 0.1 iota_compare_fusion.4
  4.0 0.1 select_reduce_fusion.1
  4.2 0.1 sub.17
  4.2 0.4 %convolution_convert_fusion.1.refs_0_ = bf16[64,2048]{1,0:T(8,128)(2,1)S(1)} fusion(bf16[384,2048]{1,0:T(8,128)(2,1)S(1)} %copy-done, s32[64]{0:T(128)S(1)} %sub.17), kind=kOutput, calls=%fused_computation.1 | convolution fusion | flops 100818944 | bytes 1835264 | tf_op jit(solution)/shard_map/dot_general | solution.py:185
  4.8 0.8 %collective-permute-done = s32[9,4,8]{2,1,0:T(4,128)S(1)} collective-permute-done((s32[9,4,8]{2,1,0:T(4,128)S(1)}, s32[9,4,8]{2,1,0:T(4,128)S(1)}, u32[]{:S(2)}, u32[]{:S(2)}) %collective-permute-start) | collective-permute-done | bytes 1184 | tf_op jit(solution)/shard_map/ppermute | solution.py:200
  5.6 0.1 select_reduce_fusion
  5.7 0.1 sub.19
  5.8 0.4 %convolution_convert_fusion = bf16[64,2048]{1,0:T(8,128)(2,1)S(1)} fusion(bf16[384,2048]{1,0:T(8,128)(2,1)S(1)} %copy-done, s32[64]{0:T(128)S(1)} %sub.19), kind=kOutput, calls=%fused_computation | convolution fusion | flops 100818944 | bytes 1835264 | tf_op jit(solution)/shard_map/dot_general | solution.py:185
  6.3 2.1 %collective-permute-start.2 = (bf16[32,2048]{1,0:T(8,128)(2,1)S(1)}, bf16[32,2048]{1,0:T(8,128)(2,1)S(1)}, u32[]{:S(2)}, u32[]{:S(2)}) collective-permute-start(bf16[32,2048]{1,0:T(8,128)(2,1)S(1)} %get-tuple-element.24), channel_id=1, source_target_pairs={{0,8},{8,0},{1,9},{9,1},{2,10},{10,2},{3,11},{11,3},{4,12},{12,4},... | collective-permute-start | bytes 393224 | tf_op jit(solution)/shard_map/ppermute | solution.py:209
  8.5 2.5 %toeplitz.1 = (bf16[64,128,512]{2,1,0:T(8,128)(2,1)S(1)}, f32[64,128]{1,0:T(8,128)S(1)}) custom-call(s32[4,8]{1,0:T(4,128)S(1)} %bitcast.27, bf16[8,4,8,300]{3,2,1,0:T(8,128)(2,1)S(1)} %copy-done.1), custom_call_target="tpu_custom_call" | custom-call | flops 10000000 | bytes 9000000 | tf_op jit(solution)/shard_map/toeplitz/pallas_call | solution.py:55
  11.0 0.1 collective-permute-start.1
  11.1 0.8 %collective-permute-done.2.refs_1_ = bf16[32,2048]{1,0:T(8,128)(2,1)S(1)} collective-permute-done((bf16[32,2048]{1,0:T(8,128)(2,1)S(1)}, bf16[32,2048]{1,0:T(8,128)(2,1)S(1)}, u32[]{:S(2)}, u32[]{:S(2)}) %collective-permute-start.2) | collective-permute-done | bytes 131104 | tf_op jit(solution)/shard_map/ppermute | solution.py:209
  11.9 2.9 %stack.49 = f32[4,24,128]{2,1,0:T(8,128)S(1)} custom-call(s32[4,8]{1,0:T(4,128)S(1)} %bitcast.28, s32[8,4,8]{2,1,0:T(4,128)S(1)} %copy-done.2, bf16[64,2048]{1,0:T(8,128)(2,1)S(1)} %convolution_convert_fusion.1.refs_0_, bf16[32,2048]{1,0:T(8,128)(2,1)S(1)} %collective-permute-done.2.refs_1_, bf16[64,128,512]{2,1,0:T(8,128)(2,1)S(1)} %get-tuple-element.22.refs_2_, ...), custom_call_target="tpu_custom_call" | custom-call | flops 200000000 | bytes 4000000 | tf_op jit(solution)/shard_map/stack/pallas_call | solution.py:146
  14.9 1.1 %collective-permute-done.1.refs_1_ = bf16[32,2048]{1,0:T(8,128)(2,1)S(1)} collective-permute-done((bf16[32,2048]{1,0:T(8,128)(2,1)S(1)}, bf16[32,2048]{1,0:T(8,128)(2,1)S(1)}, u32[]{:S(2)}, u32[]{:S(2)}) %collective-permute-start.1) | collective-permute-done | bytes 131104 | tf_op jit(solution)/shard_map/ppermute | solution.py:225
  16.0 1.9 %stack.50 = f32[2,24,128]{2,1,0:T(8,128)S(1)} custom-call(s32[4,8]{1,0:T(4,128)S(1)} %bitcast.29, s32[8,4,8]{2,1,0:T(4,128)S(1)} %copy-done.2, bf16[64,2048]{1,0:T(8,128)(2,1)S(1)} %convolution_convert_fusion.1.refs_0_, bf16[32,2048]{1,0:T(8,128)(2,1)S(1)} %collective-permute-done.1.refs_1_, bf16[64,128,512]{2,1,0:T(8,128)(2,1)S(1)} %get-tuple-element.22.refs_2_, ...), custom_call_target="tpu_custom_call" | custom-call | flops 100000000 | bytes 2000000 | tf_op jit(solution)/shard_map/stack/pallas_call | solution.py:146
  18.0 1.6 %collective-permute-start.4 = (f32[2,24,128]{2,1,0:T(8,128)S(1)}, f32[2,24,128]{2,1,0:T(8,128)S(1)}, u32[]{:S(2)}, u32[]{:S(2)}) collective-permute-start(f32[2,24,128]{2,1,0:T(8,128)S(1)} %slice_add_fusion), channel_id=1, source_target_pairs={{0,2},{1,3},{2,0},{3,1},{4,6},{5,7},{6,4},{7,5},{8,10},{9,11},{10,... | collective-permute-start | bytes 73736 | tf_op jit(solution)/shard_map/ppermute | solution.py:233
  19.6 1.9 %stack.48 = f32[2,24,128]{2,1,0:T(8,128)S(1)} custom-call(s32[4,8]{1,0:T(4,128)S(1)} %bitcast.30, s32[8,4,8]{2,1,0:T(4,128)S(1)} %copy-done.2, bf16[64,2048]{1,0:T(8,128)(2,1)S(1)} %convolution_convert_fusion.1.refs_0_, bf16[32,2048]{1,0:T(8,128)(2,1)S(1)} %collective-permute-done.1.refs_1_, bf16[64,128,512]{2,1,0:T(8,128)(2,1)S(1)} %get-tuple-element.22.refs_2_, ...), custom_call_target="tpu_custom_call" | custom-call | flops 100000000 | bytes 2000000 | tf_op jit(solution)/shard_map/stack/pallas_call | solution.py:146
  21.5 0.3 %collective-permute-done.4 = f32[2,24,128]{2,1,0:T(8,128)S(1)} collective-permute-done((f32[2,24,128]{2,1,0:T(8,128)S(1)}, f32[2,24,128]{2,1,0:T(8,128)S(1)}, u32[]{:S(2)}, u32[]{:S(2)}) %collective-permute-start.4) | collective-permute-done | bytes 24608 | tf_op jit(solution)/shard_map/ppermute | solution.py:233
  21.9 2.6 %collective-permute-start.5 = (f32[1,24,128]{2,1,0:T(8,128)S(1)}, f32[1,24,128]{2,1,0:T(8,128)S(1)}, u32[]{:S(2)}, u32[]{:S(2)}) collective-permute-start(f32[1,24,128]{2,1,0:T(8,128)S(1)} %slice.49), channel_id=1, source_target_pairs={{0,4},{1,5},{2,6},{3,7},{4,0},{5,1},{6,2},{7,3},{8,12},{9,13},{10,... | collective-permute-start | bytes 36872 | tf_op jit(solution)/shard_map/ppermute | solution.py:233
  24.5 2.0 %collective-permute-done.5 = f32[1,24,128]{2,1,0:T(8,128)S(1)} collective-permute-done((f32[1,24,128]{2,1,0:T(8,128)S(1)}, f32[1,24,128]{2,1,0:T(8,128)S(1)}, u32[]{:S(2)}, u32[]{:S(2)}) %collective-permute-start.5) | collective-permute-done | bytes 12320 | tf_op jit(solution)/shard_map/ppermute | solution.py:233
  26.5 0.6 %slice_add_fusion.3 = f32[1,24,128]{2,1,0:T(8,128)} fusion(f32[1,24,128]{2,1,0:T(8,128)S(1)} %collective-permute-done.5, f32[2,24,128]{2,1,0:T(8,128)S(1)} %fusion.5), kind=kLoop, calls=%fused_computation.18 | loop fusion | flops 3072 | bytes 36864 | tf_op jit(solution)/shard_map/add | solution.py:242
  (30 shorter events, 0.3 us)
Async XLA Ops:
  0.0 4.2 %copy-start = (bf16[384,2048]{1,0:T(8,128)(2,1)S(1)}, bf16[384,2048]{1,0:T(8,128)(2,1)}, u32[]{:S(2)}) copy-start(bf16[384,2048]{1,0:T(8,128)(2,1)} %param.5) | copy-start | bytes 4718596
  0.9 4.7 %collective-permute-start = (s32[9,4,8]{2,1,0:T(4,128)S(1)}, s32[9,4,8]{2,1,0:T(4,128)S(1)}, u32[]{:S(2)}, u32[]{:S(2)}) collective-permute-start(s32[9,4,8]{2,1,0:T(4,128)S(1)} %pad_add_fusion), channel_id=1, source_target_pairs={{0,8},{8,0},{1,9},{9,1},{2,10},{10,2},{3,11},{11,3},{4,12},{12,4},... | collective-permute-start | bytes 3464 | tf_op jit(solution)/shard_map/ppermute | solution.py:200
  4.7 3.8 %copy-start.1 = (bf16[8,4,8,300]{3,2,1,0:T(8,128)(2,1)S(1)}, bf16[8,4,8,300]{3,2,1,0:T(8,128)(2,1)}, u32[]{:S(2)}) copy-start(bf16[8,4,8,300]{3,2,1,0:T(8,128)(2,1)} %waves_ref.1) | copy-start | bytes 460804
  4.7 3.8 %copy-start.3 = (s32[8,4]{0,1:T(4,128)S(1)}, s32[8,4]{0,1:T(4,128)}, u32[]{:S(2)}) copy-start(s32[8,4]{0,1:T(4,128)} %param.7) | copy-start | bytes 388
  4.7 7.2 %copy-start.2 = (s32[8,4,8]{2,1,0:T(4,128)S(1)}, s32[8,4,8]{2,1,0:T(4,128)}, u32[]{:S(2)}) copy-start(s32[8,4,8]{2,1,0:T(4,128)} %shift_ref.5) | copy-start | bytes 3076
  6.3 5.6 %collective-permute-start.2 = (bf16[32,2048]{1,0:T(8,128)(2,1)S(1)}, bf16[32,2048]{1,0:T(8,128)(2,1)S(1)}, u32[]{:S(2)}, u32[]{:S(2)}) collective-permute-start(bf16[32,2048]{1,0:T(8,128)(2,1)S(1)} %get-tuple-element.24), channel_id=1, source_target_pairs={{0,8},{8,0},{1,9},{9,1},{2,10},{10,2},{3,11},{11,3},{4,12},{12,4},... | collective-permute-start | bytes 393224 | tf_op jit(solution)/shard_map/ppermute | solution.py:209
  11.0 5.0 %collective-permute-start.1 = (bf16[32,2048]{1,0:T(8,128)(2,1)S(1)}, bf16[32,2048]{1,0:T(8,128)(2,1)S(1)}, u32[]{:S(2)}, u32[]{:S(2)}) collective-permute-start(bf16[32,2048]{1,0:T(8,128)(2,1)S(1)} %get-tuple-element.21), channel_id=1, source_target_pairs={{0,8},{8,0},{1,9},{9,1},{2,10},{10,2},{3,11},{11,3},{4,12},{12,4},... | collective-permute-start | bytes 393224 | tf_op jit(solution)/shard_map/ppermute | solution.py:225
  14.8 3.1 %collective-permute-start.3 = (f32[4,24,128]{2,1,0:T(8,128)S(1)}, f32[4,24,128]{2,1,0:T(8,128)S(1)}, u32[]{:S(2)}, u32[]{:S(2)}) collective-permute-start(f32[4,24,128]{2,1,0:T(8,128)S(1)} %stack.49), channel_id=1, source_target_pairs={{0,1},{1,0},{2,3},{3,2},{4,5},{5,4},{6,7},{7,6},{8,9},{9,8},{10,11... | collective-permute-start | bytes 147464 | tf_op jit(solution)/shard_map/ppermute | solution.py:233
  18.0 3.9 %collective-permute-start.4 = (f32[2,24,128]{2,1,0:T(8,128)S(1)}, f32[2,24,128]{2,1,0:T(8,128)S(1)}, u32[]{:S(2)}, u32[]{:S(2)}) collective-permute-start(f32[2,24,128]{2,1,0:T(8,128)S(1)} %slice_add_fusion), channel_id=1, source_target_pairs={{0,2},{1,3},{2,0},{3,1},{4,6},{5,7},{6,4},{7,5},{8,10},{9,11},{10,... | collective-permute-start | bytes 73736 | tf_op jit(solution)/shard_map/ppermute | solution.py:233
  21.9 4.7 %collective-permute-start.5 = (f32[1,24,128]{2,1,0:T(8,128)S(1)}, f32[1,24,128]{2,1,0:T(8,128)S(1)}, u32[]{:S(2)}, u32[]{:S(2)}) collective-permute-start(f32[1,24,128]{2,1,0:T(8,128)S(1)} %slice.49), channel_id=1, source_target_pairs={{0,4},{1,5},{2,6},{3,7},{4,0},{5,1},{6,2},{7,3},{8,12},{9,13},{10,... | collective-permute-start | bytes 36872 | tf_op jit(solution)/shard_map/ppermute | solution.py:233

commit v3 on v2

v3 whole, which is shorter than its diff:
```python
import functools
import jax
import jax.numpy as jnp
from jax import lax
from jax.experimental import pallas as pl
from jax.experimental.pallas import tpu as pltpu
from jax.sharding import PartitionSpec as P

NT = 3072
LANES = 128
eps_value = 1e-05
KERNEL_VMEM = 24 << 20


def order_of(stations):
    bits = stations.bit_length() - 1
    reverse = lambda m: sum(((m >> b) & 1) << (bits - 1 - b) for b in range(bits))
    return sorted(range(stations), key=reverse, reverse=True)


def template_at(position, stations, templates, station):
    own_rows = templates // stations
    entry = order_of(stations)[position // own_rows]
    return (entry ^ station) * own_rows + position % own_rows


def toeplitz_kernel(
    slots, length, span, stations, groups_ref, shift_ref, waves_ref, tiles_ref, inv_ref, scalar_ref, padded, flipped
):
    templates = waves_ref.shape[0]
    taps = span // LANES
    rows = templates * slots
    station = lax.axis_index("stn")
    padded[...] = jnp.zeros_like(padded)
    groups = groups_ref[...]
    number = lax.broadcasted_iota(jnp.int32, groups.shape, 0)
    column = lax.broadcasted_iota(jnp.int32, groups.shape, 1)
    for p in range(templates):
        k = template_at(p, stations, templates, station)
        touch = jnp.sum(jnp.where((column == k) & (groups == station), number, 0))
        scalar_ref[p : p + 1, :] = shift_ref[k, pl.ds(touch, 1), :]
        waves = waves_ref[k, touch].astype(jnp.float32)
        power = jnp.sum(waves * waves, axis=1, keepdims=True) / length
        inv = 1.0 / (length * jnp.sqrt(power + eps_value))
        inv_ref[p * slots : (p + 1) * slots, :] = jnp.broadcast_to(inv, (slots, LANES))
        padded[p * slots : (p + 1) * slots, 0:length] = waves
    down = lax.broadcasted_iota(jnp.int32, (LANES, LANES), 0)
    along = lax.broadcasted_iota(jnp.int32, (LANES, LANES), 1)
    exchange = (down + along == LANES - 1).astype(jnp.bfloat16)
    for q in range(taps):
        block = padded[:, (taps - 1 - q) * LANES : (taps - q) * LANES].astype(jnp.bfloat16)
        flipped[:, q * LANES : (q + 1) * LANES] = jnp.dot(block, exchange, preferred_element_type=jnp.float32)
    for row in range(rows):
        turned = jnp.broadcast_to(flipped[row : row + 1, :], (LANES, span))
        turned = pltpu.roll(turned, 1, 1, stride=1, stride_axis=0).astype(jnp.bfloat16)
        for o in range(taps):
            lanes = (taps - o) % taps * LANES
            tiles_ref[row, o * LANES : (o + 1) * LANES, :] = turned[:, lanes : lanes + LANES]


def make_tiles(groups, shifts, waves, stations):
    templates, _, slots, length = waves.shape
    span = LANES * (-(-(LANES + length - 1) // LANES))
    rows = templates * slots
    vmem = pl.BlockSpec(memory_space=pltpu.VMEM)
    return pl.pallas_call(
        functools.partial(toeplitz_kernel, slots, length, span, stations),
        out_shape=(
            jax.ShapeDtypeStruct((rows, span, LANES), jnp.bfloat16),
            jax.ShapeDtypeStruct((rows, LANES), jnp.float32),
            jax.ShapeDtypeStruct((templates, slots), jnp.int32),
        ),
        in_specs=[vmem] * 3,
        out_specs=(vmem, vmem, vmem),
        scratch_shapes=[pltpu.VMEM((rows, span), jnp.float32), pltpu.VMEM((rows, span), jnp.float32)],
        name="toeplitz",
        cost_estimate=pl.CostEstimate(flops=10000000, bytes_accessed=9000000, transcendentals=0),
        compiler_params=pltpu.CompilerParams(vmem_limit_bytes=KERNEL_VMEM),
    )(groups, shifts, waves)


def stack_kernel(slots, length, blocks, positions, starts, scalar_ref, *refs):
    pieces = len(starts)
    piece_refs, refs = refs[:pieces], refs[pieces:]
    tiles_ref, inv_ref, band_ref, out_ref, raw, rolled, aligned, sums, whole = refs
    taps = tiles_ref.shape[1] // LANES
    rows = len(positions) * slots
    pitch = raw.shape[0] // rows
    wide = aligned.shape[0] // rows
    for i, piece in enumerate(piece_refs):
        start = 0
        if pieces == 2:
            me = lax.axis_index("tmpl")
            start = (me if i == 0 else 1 - me) * (piece.shape[1] // LANES)
        for a in range(piece.shape[1] // LANES):
            for r in range(0, rows, 8):
                first = starts[i] + r
                part = piece[first : first + 8, a * LANES : (a + 1) * LANES].astype(jnp.float32)
                raw[pl.ds(r * pitch + start + a, 8, stride=pitch), :] = part
    lane = lax.broadcasted_iota(jnp.int32, (wide, LANES), 1)

    scalars = scalar_ref[...]
    for i, position in enumerate(positions):
        for s in range(slots):
            row = i * slots + s
            shift = scalars[position, s]
            block = shift >> 7
            fine = shift & (LANES - 1)
            turned = pltpu.roll(raw[pl.ds(row * pitch + block, wide), :], LANES - fine, 1)
            rolled[row, 0:wide, :] = turned
            value = jnp.where(lane < LANES - fine, turned, rolled[row, pl.ds(1, wide), :])
            aligned[row * wide : (row + 1) * wide, :] = value
    value = aligned[...]
    square = value * value
    high = square.astype(jnp.bfloat16)
    low = (square - high.astype(jnp.float32)).astype(jnp.bfloat16)
    part = jnp.dot(jnp.concatenate([high, low], axis=1), band_ref[...], preferred_element_type=jnp.float32)
    sums[...] = part
    whole[...] = jnp.broadcast_to(part[:, 0:1], whole.shape)

    full, rest = length // LANES, length % LANES
    ahead = lax.broadcasted_iota(jnp.int32, (blocks, LANES), 1) < LANES - rest

    def energy_of(row):
        first = row * wide
        energy = sums[pl.ds(first, blocks), 0:LANES]
        for o in range(1, full):
            energy = energy + whole[pl.ds(first + o, blocks), :]
        near = sums[pl.ds(first + full, blocks), LANES : 2 * LANES]
        far = sums[pl.ds(first + full + 1, blocks), LANES : 2 * LANES]
        return energy + jnp.where(ahead, near, whole[pl.ds(first + full, blocks), :] + far)

    for i, position in enumerate(positions):
        total = jnp.zeros((blocks, LANES), jnp.float32)
        for s in range(0, slots, 2):
            row = i * slots + s
            window = jnp.concatenate(
                [
                    jnp.concatenate([aligned[pl.ds((row + h) * wide + o, blocks), :] for h in range(2)], axis=0)
                    for o in range(taps)
                ],
                axis=1,
            ).astype(jnp.bfloat16)
            first = position * slots + s
            tiles = jnp.concatenate([tiles_ref[first], tiles_ref[first + 1]], axis=1)
            correl = jnp.dot(window, tiles, preferred_element_type=jnp.float32)
            for h in range(2):
                weight = inv_ref[pl.ds(first + h, 1), :]
                scale = lax.rsqrt(energy_of(row + h) / length + eps_value) * weight
                total = total + correl[h * blocks : (h + 1) * blocks, h * LANES : (h + 1) * LANES] * scale
        out_ref[i] = total


def make_stacks(positions, scalars, slots, pieces, tiles, inv, band, length):
    taps = tiles.shape[1] // LANES
    rows = len(positions) * slots
    blocks = NT // LANES
    wide = 8 * (-(-(blocks + taps - 1) // 8))
    depth = sum(p.shape[1] for p, _ in pieces) // LANES
    pitch = 8 * (-(-(depth + wide - blocks) // 8))
    vmem = pl.BlockSpec(memory_space=pltpu.VMEM)
    return pl.pallas_call(
        functools.partial(stack_kernel, slots, length, blocks, positions, tuple(first for _, first in pieces)),
        out_shape=jax.ShapeDtypeStruct((len(positions), blocks, LANES), jnp.float32),
        in_specs=[vmem] * (len(pieces) + 4),
        out_specs=vmem,
        scratch_shapes=[
            pltpu.VMEM((rows * pitch, LANES), jnp.float32),
            pltpu.VMEM((rows, wide + 8, LANES), jnp.float32),
            pltpu.VMEM((rows * wide, LANES), jnp.float32),
            pltpu.VMEM((rows * wide, 2 * LANES), jnp.float32),
            pltpu.VMEM((rows * wide, LANES), jnp.float32),
        ],
        name="stack",
        cost_estimate=pl.CostEstimate(
            flops=50000000 * len(positions), bytes_accessed=1000000 * len(positions), transcendentals=0
        ),
        compiler_params=pltpu.CompilerParams(vmem_limit_bytes=KERNEL_VMEM),
    )(scalars, *[p for p, _ in pieces], tiles, inv, band)


def band_matrix(length):
    c = lax.broadcasted_iota(jnp.int32, (2 * LANES, 2 * LANES), 0) % LANES
    b = lax.broadcasted_iota(jnp.int32, (2 * LANES, 2 * LANES), 1)
    return jnp.where(b < LANES, c >= b, c < (b + length) % LANES).astype(jnp.bfloat16)


def of_station(groups, values, station, stations):
    templates = groups.shape[0]
    named = jnp.stack([template_at(p, stations, templates, station) for p in range(templates)])
    here = (groups == station)[None] & (lax.iota(jnp.int32, templates)[None] == named[:, None])[:, :, None]
    return jnp.sum(jnp.where(here[..., None], values[None], 0), axis=(1, 2))


def pick_rows(groups, offsets, station, stations, signal):
    templates, _, slots = offsets.shape
    count = signal.shape[0]
    wanted = of_station(groups, offsets + 1, station, stations) - 1
    hot = wanted[..., None] == lax.broadcasted_iota(jnp.int32, (1, 1, count), 2)
    hot = hot.reshape(templates * slots, count).astype(signal.dtype)
    return jnp.dot(hot, signal, preferred_element_type=jnp.float32).astype(signal.dtype)


def shards(signal, waveforms, station_groups, channel_offsets, moveouts):
    templates, touches, slots, length = waveforms.shape
    samples = signal.shape[1]
    parts = lax.axis_size("tmpl")
    stations = lax.axis_size("stn")
    station = lax.axis_index("stn")
    groups = station_groups.T
    half, quarter = templates // 2, templates // 4
    if parts == 2:
        swap = [(0, 1), (1, 0)]
        if templates == slots:
            packed = lax.optimization_barrier(jnp.concatenate([channel_offsets, groups[None]], axis=0))
            named, asked = [(x[templates].T, x[:templates]) for x in (packed, lax.ppermute(packed, "tmpl", swap))]
        else:
            named = station_groups, channel_offsets
            asked = [lax.ppermute(x, "tmpl", swap) for x in named]
        own = pick_rows(*named, station, stations, signal)
        asked, own = lax.optimization_barrier((asked, own))
        sent = pick_rows(*asked, station, stations, signal)
        sent, groups = lax.optimization_barrier((sent, groups))
        got = lax.ppermute(sent, "tmpl", swap)

        def pieces(first):
            return (own, first * slots), (got, first * slots)
    else:
        asked = [lax.all_gather(x, "tmpl", axis=0) for x in (station_groups, channel_offsets)]
        sent = jnp.stack([pick_rows(asked[0][i], asked[1][i], station, stations, signal) for i in range(parts)])
        got = lax.all_to_all(sent, "tmpl", split_axis=0, concat_axis=0, tiled=True)
        got = got.transpose(1, 0, 2).reshape(templates * slots, parts * samples)

        def pieces(first):
            return ((got, first * slots),)

    tiles, inv, scalars = make_tiles(groups, moveouts, waveforms, stations)
    band = band_matrix(length)

    def stacks(first, last):
        positions = tuple(range(first, last))
        return make_stacks(positions, scalars, slots, pieces(first), tiles, inv, band, length)

    def across(x, step):
        return lax.ppermute(x, "stn", [(j, j ^ step) for j in range(stations)])

    came = across(stacks(0, half), 1)
    left = stacks(half, half + quarter) + came[:quarter]
    came_left = across(left, 2)
    total = stacks(half + quarter, templates) + came[quarter:] + came_left
    step = 4
    while step < stations:
        middle = total.shape[0] // 2
        total = total[middle:] + across(total[:middle], step)
        step *= 2
    return total.reshape(templates // stations, NT)


def solution(mesh):
    in_specs = (
        P("stn", ("span", "tmpl")),
        P("tmpl", None, None, None),
        P("tmpl", None),
        P("tmpl", None, None),
        P("tmpl", None, None),
    )
    out_specs = P(("tmpl", "stn"), "span")
    return jax.shard_map(shards, mesh=mesh, in_specs=in_specs, out_specs=out_specs, check_vma=False)
```

time: 27.4 us -> 25.5 us (0.931)
  Pallas kernels: 9.27 us -> 5.35 us
  waiting for transfers between devices: 5.06 us -> 6.75 us
  starting transfers between devices: 9.47 us -> 9.85 us
    pallas_call x3, Pallas kernels: 6.8 us -> 2.84 us  [make_stacks(): pl.pallas_call(functools.partial(stack_kernel, slots, length, blocks, pos...]
    ppermute x3, waiting for transfers between devices: 2.32 us -> 3.5 us  [across(): return lax.ppermute(x, 'stn', [(j, j ^ step) for j in range(stations)])]
    ppermute x3, starting transfers between devices: 4.33 us -> 4.79 us  [across(): return lax.ppermute(x, 'stn', [(j, j ^ step) for j in range(stations)])]
    ppermute x2 -> x1, waiting for transfers between devices: 1.96 us -> 2.42 us  [shards(): got = lax.ppermute(sent, 'tmpl', swap)]
    ppermute x2 -> x1, starting transfers between devices: 2.18 us -> 2.09 us  [shards(): got = lax.ppermute(sent, 'tmpl', swap)]
  transfers between devices with their start and end apart: 6 -> 5, of which waited for: 5 -> 5; matrix products, arithmetic and copies ran while one was open for 4% -> 4% of each run, Pallas kernels for 34% -> 16%
where the time goes in v3:
time: 25.5 us; the launch traced here: 25.3 us
  starting transfers between devices  9.85 us (39%)
  waiting for transfers between devices  6.75 us (26%)
  Pallas kernels  5.35 us (21%)
  other arithmetic  2.01 us (8%)
  matrix products  0.87 us (3%)
  local copies, waits for them, and re-layouts  0.28 us (1%)
    ppermute x3, starting transfers between devices, across(): return lax.ppermute(x, 'stn', [(j, j ^ step) for j in range(stations)])  4.79 us
    ppermute x3, waiting for transfers between devices, across(): return lax.ppermute(x, 'stn', [(j, j ^ step) for j in range(stations)])  3.5 us
    ppermute x1, starting transfers between devices, shards(): lax.ppermute(packed, 'tmpl', swap)  2.97 us
    pallas_call x3, Pallas kernels, make_stacks(): pl.pallas_call(functools.partial(stack_kernel, slots, length, blocks, pos...  2.84 us
    pallas_call x1, Pallas kernels, make_tiles(): pl.pallas_call(functools.partial(toeplitz_kernel, slots, length, span, st...  2.52 us
    ppermute x1, waiting for transfers between devices, shards(): got = lax.ppermute(sent, 'tmpl', swap)  2.42 us
    ppermute x1, starting transfers between devices, shards(): got = lax.ppermute(sent, 'tmpl', swap)  2.09 us
    dot_general x2, matrix products, pick_rows(): jnp.dot(hot, signal, preferred_element_type=jnp.float32)  0.87 us
  transfers between devices with their start and end apart: 5, of which 5 were waited for; matrix products, arithmetic and copies ran while one was open for 4% of the time, Pallas kernels for 16%

profile of v3, /device:TPU:0, one launch (start us, length us, event | category | flops | bytes accessed | tf_op | source)
XLA Modules:
  0.0 25.3 jit_solution(11482612998543600141)
XLA Ops:
  0.0 0.9 %pad_add_fusion = s32[9,4,8]{2,1,0:T(4,128)S(1)} fusion(s32[1,4,8]{2,1,0:T(4,128)} %bitcast.22, s32[8,4,8]{2,1,0:T(4,128)} %param.8), kind=kLoop, calls=%fused_computation.15 | loop fusion | flops 288 | bytes 2304 | tf_op jit(solution)/shard_map/concatenate | solution.py:215
  0.9 3.0 %collective-permute-start = (s32[9,4,8]{2,1,0:T(4,128)S(1)}, s32[9,4,8]{2,1,0:T(4,128)S(1)}, u32[]{:S(2)}, u32[]{:S(2)}) collective-permute-start(s32[9,4,8]{2,1,0:T(4,128)S(1)} %pad_add_fusion), channel_id=1, source_target_pairs={{0,8},{8,0},{1,9},{9,1},{2,10},{10,2},{3,11},{11,3},{4,12},{12,4},... | collective-permute-start | bytes 3464 | tf_op jit(solution)/shard_map/ppermute | solution.py:216
  3.9 0.1 stack.47
  4.0 0.1 iota_compare_fusion.4
  4.0 0.1 select_reduce_fusion.1
  4.2 0.1 sub.11
  4.3 0.4 %convolution_convert_fusion.1.refs_0_ = bf16[64,2048]{1,0:T(8,128)(2,1)S(1)} fusion(bf16[384,2048]{1,0:T(8,128)(2,1)S(1)} %copy-done, s32[64]{0:T(128)S(1)} %sub.11), kind=kOutput, calls=%fused_computation.1 | convolution fusion | flops 100818944 | bytes 1835264 | tf_op jit(solution)/shard_map/dot_general | solution.py:201
  4.7 0.8 %collective-permute-done = s32[9,4,8]{2,1,0:T(4,128)S(1)} collective-permute-done((s32[9,4,8]{2,1,0:T(4,128)S(1)}, s32[9,4,8]{2,1,0:T(4,128)S(1)}, u32[]{:S(2)}, u32[]{:S(2)}) %collective-permute-start) | collective-permute-done | bytes 1184 | tf_op jit(solution)/shard_map/ppermute | solution.py:216
  5.6 0.1 select_reduce_fusion
  5.7 0.1 sub.13
  5.8 0.4 %convolution_convert_fusion = bf16[64,2048]{1,0:T(8,128)(2,1)S(1)} fusion(bf16[384,2048]{1,0:T(8,128)(2,1)S(1)} %copy-done, s32[64]{0:T(128)S(1)} %sub.13), kind=kOutput, calls=%fused_computation | convolution fusion | flops 100818944 | bytes 1835264 | tf_op jit(solution)/shard_map/dot_general | solution.py:201
  6.3 2.1 %collective-permute-start.1 = (bf16[64,2048]{1,0:T(8,128)(2,1)S(1)}, bf16[64,2048]{1,0:T(8,128)(2,1)S(1)}, u32[]{:S(2)}, u32[]{:S(2)}) collective-permute-start(bf16[64,2048]{1,0:T(8,128)(2,1)S(1)} %convolution_convert_fusion), channel_id=1, source_target_pairs={{0,8},{8,0},{1,9},{9,1},{2,10},{10,2},{3,11},{11,3},{4,12},{12,4},... | collective-permute-start | bytes 786440 | tf_op jit(solution)/shard_map/ppermute | solution.py:224
  8.4 0.2 fusion.1.refs_4_
  8.6 2.5 %toeplitz.1 = (bf16[64,512,128]{2,1,0:T(8,128)(2,1)S(1)}, f32[64,128]{1,0:T(8,128)S(1)}, s32[8,8]{1,0:T(8,128)S(1)}) custom-call(s32[4,8]{1,0:T(4,128)S(1)} %bitcast.23, s32[8,4,8]{2,1,0:T(4,128)S(1)} %copy-done.2, bf16[8,4,8,300]{3,2,1,0:T(8,128)(2,1)S(1)} %copy-done.1), custom_call_target="tpu_custom_call" | custom-call | flops 10000000 | bytes 9000000 | tf_op jit(solution)/shard_map/toeplitz/pallas_call | solution.py:66
  11.1 2.4 %collective-permute-done.1.refs_1_ = bf16[64,2048]{1,0:T(8,128)(2,1)S(1)} collective-permute-done((bf16[64,2048]{1,0:T(8,128)(2,1)S(1)}, bf16[64,2048]{1,0:T(8,128)(2,1)S(1)}, u32[]{:S(2)}, u32[]{:S(2)}) %collective-permute-start.1) | collective-permute-done | bytes 262176 | tf_op jit(solution)/shard_map/ppermute | solution.py:224
  13.5 1.4 %stack.49 = f32[4,24,128]{2,1,0:T(8,128)S(1)} custom-call(s32[8,8]{1,0:T(8,128)S(1)} %get-tuple-element.16.scalar_ref, bf16[64,2048]{1,0:T(8,128)(2,1)S(1)} %convolution_convert_fusion.1.refs_0_, bf16[64,2048]{1,0:T(8,128)(2,1)S(1)} %collective-permute-done.1.refs_1_, bf16[64,512,128]{2,1,0:T(8,128)(2,1)S(1)} %get-tuple-element.19.refs_2_, ...), custom_call_target="tpu_custom_call" | custom-call | flops 200000000 | bytes 4000000 | tf_op jit(solution)/shard_map/stack/pallas_call | solution.py:162
  15.0 0.7 %stack.50 = f32[2,24,128]{2,1,0:T(8,128)S(1)} custom-call(s32[8,8]{1,0:T(8,128)S(1)} %get-tuple-element.16.scalar_ref, bf16[64,2048]{1,0:T(8,128)(2,1)S(1)} %convolution_convert_fusion.1.refs_0_, bf16[64,2048]{1,0:T(8,128)(2,1)S(1)} %collective-permute-done.1.refs_1_, bf16[64,512,128]{2,1,0:T(8,128)(2,1)S(1)} %get-tuple-element.19.refs_2_, ...), custom_call_target="tpu_custom_call" | custom-call | flops 100000000 | bytes 2000000 | tf_op jit(solution)/shard_map/stack/pallas_call | solution.py:162
  15.7 0.5 %collective-permute-done.2 = f32[4,24,128]{2,1,0:T(8,128)S(1)} collective-permute-done((f32[4,24,128]{2,1,0:T(8,128)S(1)}, f32[4,24,128]{2,1,0:T(8,128)S(1)}, u32[]{:S(2)}, u32[]{:S(2)}) %collective-permute-start.2) | collective-permute-done | bytes 49184 | tf_op jit(solution)/shard_map/ppermute | solution.py:245
  16.2 1.8 %collective-permute-start.3 = (f32[2,24,128]{2,1,0:T(8,128)S(1)}, f32[2,24,128]{2,1,0:T(8,128)S(1)}, u32[]{:S(2)}, u32[]{:S(2)}) collective-permute-start(f32[2,24,128]{2,1,0:T(8,128)S(1)} %slice_add_fusion), channel_id=1, source_target_pairs={{0,2},{1,3},{2,0},{3,1},{4,6},{5,7},{6,4},{7,5},{8,10},{9,11},{10,... | collective-permute-start | bytes 73736 | tf_op jit(solution)/shard_map/ppermute | solution.py:245
  18.0 0.7 %stack.48 = f32[2,24,128]{2,1,0:T(8,128)S(1)} custom-call(s32[8,8]{1,0:T(8,128)S(1)} %get-tuple-element.16.scalar_ref, bf16[64,2048]{1,0:T(8,128)(2,1)S(1)} %convolution_convert_fusion.1.refs_0_, bf16[64,2048]{1,0:T(8,128)(2,1)S(1)} %collective-permute-done.1.refs_1_, bf16[64,512,128]{2,1,0:T(8,128)(2,1)S(1)} %get-tuple-element.19.refs_2_, ...), custom_call_target="tpu_custom_call" | custom-call | flops 100000000 | bytes 2000000 | tf_op jit(solution)/shard_map/stack/pallas_call | solution.py:162
  18.8 1.3 %collective-permute-done.3 = f32[2,24,128]{2,1,0:T(8,128)S(1)} collective-permute-done((f32[2,24,128]{2,1,0:T(8,128)S(1)}, f32[2,24,128]{2,1,0:T(8,128)S(1)}, u32[]{:S(2)}, u32[]{:S(2)}) %collective-permute-start.3) | collective-permute-done | bytes 24608 | tf_op jit(solution)/shard_map/ppermute | solution.py:245
  20.0 2.9 %collective-permute-start.4 = (f32[1,24,128]{2,1,0:T(8,128)S(1)}, f32[1,24,128]{2,1,0:T(8,128)S(1)}, u32[]{:S(2)}, u32[]{:S(2)}) collective-permute-start(f32[1,24,128]{2,1,0:T(8,128)S(1)} %slice.39), channel_id=1, source_target_pairs={{0,4},{1,5},{2,6},{3,7},{4,0},{5,1},{6,2},{7,3},{8,12},{9,13},{10,... | collective-permute-start | bytes 36872 | tf_op jit(solution)/shard_map/ppermute | solution.py:245
  22.9 1.8 %collective-permute-done.4 = f32[1,24,128]{2,1,0:T(8,128)S(1)} collective-permute-done((f32[1,24,128]{2,1,0:T(8,128)S(1)}, f32[1,24,128]{2,1,0:T(8,128)S(1)}, u32[]{:S(2)}, u32[]{:S(2)}) %collective-permute-start.4) | collective-permute-done | bytes 12320 | tf_op jit(solution)/shard_map/ppermute | solution.py:245
  24.7 0.6 %slice_add_fusion.3 = f32[1,24,128]{2,1,0:T(8,128)} fusion(f32[1,24,128]{2,1,0:T(8,128)S(1)} %collective-permute-done.4, f32[2,24,128]{2,1,0:T(8,128)S(1)} %fusion.4), kind=kLoop, calls=%fused_computation.17 | loop fusion | flops 3072 | bytes 36864 | tf_op jit(solution)/shard_map/add | solution.py:254
  (28 shorter events, 0.2 us)
Async XLA Ops:
  0.0 4.3 %copy-start = (bf16[384,2048]{1,0:T(8,128)(2,1)S(1)}, bf16[384,2048]{1,0:T(8,128)(2,1)}, u32[]{:S(2)}) copy-start(bf16[384,2048]{1,0:T(8,128)(2,1)} %param.5) | copy-start | bytes 4718596
  0.9 4.7 %collective-permute-start = (s32[9,4,8]{2,1,0:T(4,128)S(1)}, s32[9,4,8]{2,1,0:T(4,128)S(1)}, u32[]{:S(2)}, u32[]{:S(2)}) collective-permute-start(s32[9,4,8]{2,1,0:T(4,128)S(1)} %pad_add_fusion), channel_id=1, source_target_pairs={{0,8},{8,0},{1,9},{9,1},{2,10},{10,2},{3,11},{11,3},{4,12},{12,4},... | collective-permute-start | bytes 3464 | tf_op jit(solution)/shard_map/ppermute | solution.py:216
  4.3 4.3 %copy-start.1 = (bf16[8,4,8,300]{3,2,1,0:T(8,128)(2,1)S(1)}, bf16[8,4,8,300]{3,2,1,0:T(8,128)(2,1)}, u32[]{:S(2)}) copy-start(bf16[8,4,8,300]{3,2,1,0:T(8,128)(2,1)} %waves_ref.1) | copy-start | bytes 460804
  4.3 4.3 %copy-start.2 = (s32[8,4,8]{2,1,0:T(4,128)S(1)}, s32[8,4,8]{2,1,0:T(4,128)}, u32[]{:S(2)}) copy-start(s32[8,4,8]{2,1,0:T(4,128)} %shift_ref.1) | copy-start | bytes 3076
  4.3 4.3 %copy-start.3 = (s32[8,4]{0,1:T(4,128)S(1)}, s32[8,4]{0,1:T(4,128)}, u32[]{:S(2)}) copy-start(s32[8,4]{0,1:T(4,128)} %param.7) | copy-start | bytes 388
  6.3 7.2 %collective-permute-start.1 = (bf16[64,2048]{1,0:T(8,128)(2,1)S(1)}, bf16[64,2048]{1,0:T(8,128)(2,1)S(1)}, u32[]{:S(2)}, u32[]{:S(2)}) collective-permute-start(bf16[64,2048]{1,0:T(8,128)(2,1)S(1)} %convolution_convert_fusion), channel_id=1, source_target_pairs={{0,8},{8,0},{1,9},{9,1},{2,10},{10,2},{3,11},{11,3},{4,12},{12,4},... | collective-permute-start | bytes 786440 | tf_op jit(solution)/shard_map/ppermute | solution.py:224
  14.9 1.3 %collective-permute-start.2 = (f32[4,24,128]{2,1,0:T(8,128)S(1)}, f32[4,24,128]{2,1,0:T(8,128)S(1)}, u32[]{:S(2)}, u32[]{:S(2)}) collective-permute-start(f32[4,24,128]{2,1,0:T(8,128)S(1)} %stack.49), channel_id=1, source_target_pairs={{0,1},{1,0},{2,3},{3,2},{4,5},{5,4},{6,7},{7,6},{8,9},{9,8},{10,11... | collective-permute-start | bytes 147464 | tf_op jit(solution)/shard_map/ppermute | solution.py:245
  16.2 3.8 %collective-permute-start.3 = (f32[2,24,128]{2,1,0:T(8,128)S(1)}, f32[2,24,128]{2,1,0:T(8,128)S(1)}, u32[]{:S(2)}, u32[]{:S(2)}) collective-permute-start(f32[2,24,128]{2,1,0:T(8,128)S(1)} %slice_add_fusion), channel_id=1, source_target_pairs={{0,2},{1,3},{2,0},{3,1},{4,6},{5,7},{6,4},{7,5},{8,10},{9,11},{10,... | collective-permute-start | bytes 73736 | tf_op jit(solution)/shard_map/ppermute | solution.py:245
  20.0 4.7 %collective-permute-start.4 = (f32[1,24,128]{2,1,0:T(8,128)S(1)}, f32[1,24,128]{2,1,0:T(8,128)S(1)}, u32[]{:S(2)}, u32[]{:S(2)}) collective-permute-start(f32[1,24,128]{2,1,0:T(8,128)S(1)} %slice.39), channel_id=1, source_target_pairs={{0,4},{1,5},{2,6},{3,7},{4,0},{5,1},{6,2},{7,3},{8,12},{9,13},{10,... | collective-permute-start | bytes 36872 | tf_op jit(solution)/shard_map/ppermute | solution.py:245

commit v4 on v3

--- a/solution.py
+++ b/solution.py
@@ -157,7 +157,7 @@
     blocks = NT // LANES
     wide = 8 * (-(-(blocks + taps - 1) // 8))
     depth = sum(p.shape[1] for p, _ in pieces) // LANES
-    pitch = 8 * (-(-(depth + wide - blocks) // 8))
+    pitch = 8 * (-(-(depth + wide - blocks) // 8)) + 1
     vmem = pl.BlockSpec(memory_space=pltpu.VMEM)
     return pl.pallas_call(
         functools.partial(stack_kernel, slots, length, blocks, positions, tuple(first for _, first in pieces)),
@@ -195,14 +195,14 @@
 def pick_rows(groups, offsets, station, stations, signal):
     templates, _, slots = offsets.shape
     count = signal.shape[0]
-    wanted = of_station(groups, offsets + 1, station, stations) - 1
-    hot = wanted[..., None] == lax.broadcasted_iota(jnp.int32, (1, 1, count), 2)
+    wanted = of_station(groups, offsets + 1, station, stations)
+    hot = wanted[..., None] == 1 + lax.broadcasted_iota(jnp.int32, (1, 1, count), 2)
     hot = hot.reshape(templates * slots, count).astype(signal.dtype)
     return jnp.dot(hot, signal, preferred_element_type=jnp.float32).astype(signal.dtype)
 
 
 def shards(signal, waveforms, station_groups, channel_offsets, moveouts):
-    templates, touches, slots, length = waveforms.shape
+    templates, _, slots, length = waveforms.shape
     samples = signal.shape[1]
     parts = lax.axis_size("tmpl")
     stations = lax.axis_size("stn")
@@ -237,17 +237,20 @@
     tiles, inv, scalars = make_tiles(groups, moveouts, waveforms, stations)
     band = band_matrix(length)
 
-    def stacks(first, last):
+    def stacks(first, last, inv):
         positions = tuple(range(first, last))
         return make_stacks(positions, scalars, slots, pieces(first), tiles, inv, band, length)
 
     def across(x, step):
         return lax.ppermute(x, "stn", [(j, j ^ step) for j in range(stations)])
 
-    came = across(stacks(0, half), 1)
-    left = stacks(half, half + quarter) + came[:quarter]
+    came = across(stacks(0, quarter, inv), 1)
+    left = stacks(half, half + quarter, inv) + came
     came_left = across(left, 2)
-    total = stacks(half + quarter, templates) + came[quarter:] + came_left
+    away = stacks(quarter, half, inv)
+    came = across(away, 1)
+    kept = stacks(half + quarter, templates, inv)
+    total = kept + came + came_left
     step = 4
     while step < stations:
         middle = total.shape[0] // 2

time: 25.5 us -> 25.8 us (1.012)
  starting transfers between devices: 9.85 us -> 10.5 us
  waiting for transfers between devices: 6.75 us -> 6.26 us
    ppermute x3 -> x4, starting transfers between devices: 4.79 us -> 5.42 us  [across(): return lax.ppermute(x, 'stn', [(j, j ^ step) for j in range(stations)])]
    ppermute x3 -> x4, waiting for transfers between devices: 3.5 us -> 3.02 us  [across(): return lax.ppermute(x, 'stn', [(j, j ^ step) for j in range(stations)])]
    pallas_call x3 -> x4, Pallas kernels: 2.84 us -> 2.93 us  [make_stacks(): pl.pallas_call(functools.partial(stack_kernel, slots, length, blocks, pos...]
  transfers between devices with their start and end apart: 5 -> 6, of which waited for: 5 -> 4; matrix products, arithmetic and copies ran while one was open for 4% -> 4% of each run, Pallas kernels for 16% -> 18%
where the time goes in v4:
time: 25.8 us; the launch traced here: 25.6 us
  starting transfers between devices  10.5 us (41%)
  waiting for transfers between devices  6.26 us (24%)
  Pallas kernels  5.45 us (21%)
  other arithmetic  2 us (8%)
  matrix products  0.87 us (3%)
  local copies, waits for them, and re-layouts  0.28 us (1%)
    ppermute x4, starting transfers between devices, across(): return lax.ppermute(x, 'stn', [(j, j ^ step) for j in range(stations)])  5.42 us
    ppermute x4, waiting for transfers between devices, across(): return lax.ppermute(x, 'stn', [(j, j ^ step) for j in range(stations)])  3.02 us
    ppermute x1, starting transfers between devices, shards(): lax.ppermute(packed, 'tmpl', swap)  2.97 us
    pallas_call x4, Pallas kernels, make_stacks(): pl.pallas_call(functools.partial(stack_kernel, slots, length, blocks, pos...  2.93 us
    pallas_call x1, Pallas kernels, make_tiles(): pl.pallas_call(functools.partial(toeplitz_kernel, slots, length, span, st...  2.52 us
    ppermute x1, waiting for transfers between devices, shards(): got = lax.ppermute(sent, 'tmpl', swap)  2.42 us
    ppermute x1, starting transfers between devices, shards(): got = lax.ppermute(sent, 'tmpl', swap)  2.09 us
    dot_general x2, matrix products, pick_rows(): jnp.dot(hot, signal, preferred_element_type=jnp.float32)  0.87 us
  transfers between devices with their start and end apart: 6, of which 4 were waited for; matrix products, arithmetic and copies ran while one was open for 4% of the time, Pallas kernels for 18%

profile of v4, /device:TPU:0, one launch (start us, length us, event | category | flops | bytes accessed | tf_op | source)
XLA Modules:
  0.0 25.6 jit_solution(5451768647553361059)
XLA Ops:
  0.0 0.9 %pad_add_fusion = s32[9,4,8]{2,1,0:T(4,128)S(1)} fusion(s32[1,4,8]{2,1,0:T(4,128)} %bitcast.22, s32[8,4,8]{2,1,0:T(4,128)} %param.8), kind=kLoop, calls=%fused_computation.15 | loop fusion | flops 288 | bytes 2304 | tf_op jit(solution)/shard_map/concatenate | solution.py:215
  0.9 3.0 %collective-permute-start = (s32[9,4,8]{2,1,0:T(4,128)S(1)}, s32[9,4,8]{2,1,0:T(4,128)S(1)}, u32[]{:S(2)}, u32[]{:S(2)}) collective-permute-start(s32[9,4,8]{2,1,0:T(4,128)S(1)} %pad_add_fusion), channel_id=1, source_target_pairs={{0,8},{8,0},{1,9},{9,1},{2,10},{10,2},{3,11},{11,3},{4,12},{12,4},... | collective-permute-start | bytes 3464 | tf_op jit(solution)/shard_map/ppermute | solution.py:216
  3.9 0.1 stack.48
  4.1 0.1 select_reduce_fusion.1
  4.2 0.1 eq.84
  4.3 0.4 %convolution_convert_fusion.1.refs_0_ = bf16[64,2048]{1,0:T(8,128)(2,1)S(1)} fusion(bf16[384,2048]{1,0:T(8,128)(2,1)S(1)} %copy-done, s32[384]{0:T(512)S(1)} %iota_add_fusion, s32[64]{0:T(128)S(1)} %eq.84), kind=kOutput, calls=%fused_computation.1 | convolution fusion | flops 100818944 | bytes 1836800 | tf_op jit(solution)/shard_map/dot_general | solution.py:201
  4.7 0.8 %collective-permute-done = s32[9,4,8]{2,1,0:T(4,128)S(1)} collective-permute-done((s32[9,4,8]{2,1,0:T(4,128)S(1)}, s32[9,4,8]{2,1,0:T(4,128)S(1)}, u32[]{:S(2)}, u32[]{:S(2)}) %collective-permute-start) | collective-permute-done | bytes 1184 | tf_op jit(solution)/shard_map/ppermute | solution.py:216
  5.6 0.1 select_reduce_fusion
  5.7 0.1 eq.90
  5.8 0.4 %convolution_convert_fusion = bf16[64,2048]{1,0:T(8,128)(2,1)S(1)} fusion(bf16[384,2048]{1,0:T(8,128)(2,1)S(1)} %copy-done, s32[384]{0:T(512)S(1)} %iota_add_fusion, s32[64]{0:T(128)S(1)} %eq.90), kind=kOutput, calls=%fused_computation | convolution fusion | flops 100818944 | bytes 1836800 | tf_op jit(solution)/shard_map/dot_general | solution.py:201
  6.3 2.1 %collective-permute-start.1 = (bf16[64,2048]{1,0:T(8,128)(2,1)S(1)}, bf16[64,2048]{1,0:T(8,128)(2,1)S(1)}, u32[]{:S(2)}, u32[]{:S(2)}) collective-permute-start(bf16[64,2048]{1,0:T(8,128)(2,1)S(1)} %convolution_convert_fusion), channel_id=1, source_target_pairs={{0,8},{8,0},{1,9},{9,1},{2,10},{10,2},{3,11},{11,3},{4,12},{12,4},... | collective-permute-start | bytes 786440 | tf_op jit(solution)/shard_map/ppermute | solution.py:224
  8.4 0.2 fusion.1.refs_4_
  8.6 2.5 %toeplitz.1 = (bf16[64,512,128]{2,1,0:T(8,128)(2,1)S(1)}, f32[64,128]{1,0:T(8,128)S(1)}, s32[8,8]{1,0:T(8,128)S(1)}) custom-call(s32[4,8]{1,0:T(4,128)S(1)} %bitcast.23, s32[8,4,8]{2,1,0:T(4,128)S(1)} %copy-done.2, bf16[8,4,8,300]{3,2,1,0:T(8,128)(2,1)S(1)} %copy-done.1), custom_call_target="tpu_custom_call" | custom-call | flops 10000000 | bytes 9000000 | tf_op jit(solution)/shard_map/toeplitz/pallas_call | solution.py:66
  11.1 2.4 %collective-permute-done.1.refs_1_ = bf16[64,2048]{1,0:T(8,128)(2,1)S(1)} collective-permute-done((bf16[64,2048]{1,0:T(8,128)(2,1)S(1)}, bf16[64,2048]{1,0:T(8,128)(2,1)S(1)}, u32[]{:S(2)}, u32[]{:S(2)}) %collective-permute-start.1) | collective-permute-done | bytes 262176 | tf_op jit(solution)/shard_map/ppermute | solution.py:224
  13.5 0.7 %stack.52 = f32[2,24,128]{2,1,0:T(8,128)S(1)} custom-call(s32[8,8]{1,0:T(8,128)S(1)} %get-tuple-element.16.scalar_ref, bf16[64,2048]{1,0:T(8,128)(2,1)S(1)} %convolution_convert_fusion.1.refs_0_, bf16[64,2048]{1,0:T(8,128)(2,1)S(1)} %collective-permute-done.1.refs_1_, bf16[64,512,128]{2,1,0:T(8,128)(2,1)S(1)} %get-tuple-element.19.refs_2_, ...), custom_call_target="tpu_custom_call" | custom-call | flops 100000000 | bytes 2000000 | tf_op jit(solution)/shard_map/stack/pallas_call | solution.py:162
  14.3 0.7 %stack.50 = f32[2,24,128]{2,1,0:T(8,128)S(1)} custom-call(s32[8,8]{1,0:T(8,128)S(1)} %get-tuple-element.16.scalar_ref, bf16[64,2048]{1,0:T(8,128)(2,1)S(1)} %convolution_convert_fusion.1.refs_0_, bf16[64,2048]{1,0:T(8,128)(2,1)S(1)} %collective-permute-done.1.refs_1_, bf16[64,512,128]{2,1,0:T(8,128)(2,1)S(1)} %get-tuple-element.19.refs_2_, ...), custom_call_target="tpu_custom_call" | custom-call | flops 100000000 | bytes 2000000 | tf_op jit(solution)/shard_map/stack/pallas_call | solution.py:162
  15.1 0.6 %collective-permute-start.2 = (f32[2,24,128]{2,1,0:T(8,128)S(1)}, f32[2,24,128]{2,1,0:T(8,128)S(1)}, u32[]{:S(2)}, u32[]{:S(2)}) collective-permute-start(f32[2,24,128]{2,1,0:T(8,128)S(1)} %stack.50), channel_id=1, source_target_pairs={{0,1},{1,0},{2,3},{3,2},{4,5},{5,4},{6,7},{7,6},{8,9},{9,8},{10,11... | collective-permute-start | bytes 73736 | tf_op jit(solution)/shard_map/ppermute | solution.py:245
  15.6 0.7 %stack.51 = f32[2,24,128]{2,1,0:T(8,128)S(1)} custom-call(s32[8,8]{1,0:T(8,128)S(1)} %get-tuple-element.16.scalar_ref, bf16[64,2048]{1,0:T(8,128)(2,1)S(1)} %convolution_convert_fusion.1.refs_0_, bf16[64,2048]{1,0:T(8,128)(2,1)S(1)} %collective-permute-done.1.refs_1_, bf16[64,512,128]{2,1,0:T(8,128)(2,1)S(1)} %get-tuple-element.19.refs_2_, ...), custom_call_target="tpu_custom_call" | custom-call | flops 100000000 | bytes 2000000 | tf_op jit(solution)/shard_map/stack/pallas_call | solution.py:162
  16.4 1.9 %collective-permute-start.4 = (f32[2,24,128]{2,1,0:T(8,128)S(1)}, f32[2,24,128]{2,1,0:T(8,128)S(1)}, u32[]{:S(2)}, u32[]{:S(2)}) collective-permute-start(f32[2,24,128]{2,1,0:T(8,128)S(1)} %add.74), channel_id=1, source_target_pairs={{0,2},{1,3},{2,0},{3,1},{4,6},{5,7},{6,4},{7,5},{8,10},{9,11},{10,... | collective-permute-start | bytes 73736 | tf_op jit(solution)/shard_map/ppermute | solution.py:245
  18.3 0.7 %stack.49 = f32[2,24,128]{2,1,0:T(8,128)S(1)} custom-call(s32[8,8]{1,0:T(8,128)S(1)} %get-tuple-element.16.scalar_ref, bf16[64,2048]{1,0:T(8,128)(2,1)S(1)} %convolution_convert_fusion.1.refs_0_, bf16[64,2048]{1,0:T(8,128)(2,1)S(1)} %collective-permute-done.1.refs_1_, bf16[64,512,128]{2,1,0:T(8,128)(2,1)S(1)} %get-tuple-element.19.refs_2_, ...), custom_call_target="tpu_custom_call" | custom-call | flops 100000000 | bytes 2000000 | tf_op jit(solution)/shard_map/stack/pallas_call | solution.py:162
  19.0 1.3 %collective-permute-done.4 = f32[2,24,128]{2,1,0:T(8,128)S(1)} collective-permute-done((f32[2,24,128]{2,1,0:T(8,128)S(1)}, f32[2,24,128]{2,1,0:T(8,128)S(1)}, u32[]{:S(2)}, u32[]{:S(2)}) %collective-permute-start.4) | collective-permute-done | bytes 24608 | tf_op jit(solution)/shard_map/ppermute | solution.py:245
  20.3 2.9 %collective-permute-start.5 = (f32[1,24,128]{2,1,0:T(8,128)S(1)}, f32[1,24,128]{2,1,0:T(8,128)S(1)}, u32[]{:S(2)}, u32[]{:S(2)}) collective-permute-start(f32[1,24,128]{2,1,0:T(8,128)S(1)} %slice.29), channel_id=1, source_target_pairs={{0,4},{1,5},{2,6},{3,7},{4,0},{5,1},{6,2},{7,3},{8,12},{9,13},{10,... | collective-permute-start | bytes 36872 | tf_op jit(solution)/shard_map/ppermute | solution.py:245
  23.2 1.8 %collective-permute-done.5 = f32[1,24,128]{2,1,0:T(8,128)S(1)} collective-permute-done((f32[1,24,128]{2,1,0:T(8,128)S(1)}, f32[1,24,128]{2,1,0:T(8,128)S(1)}, u32[]{:S(2)}, u32[]{:S(2)}) %collective-permute-start.5) | collective-permute-done | bytes 12320 | tf_op jit(solution)/shard_map/ppermute | solution.py:245
  24.9 0.6 %slice_add_fusion.1 = f32[1,24,128]{2,1,0:T(8,128)} fusion(f32[1,24,128]{2,1,0:T(8,128)S(1)} %collective-permute-done.5, f32[2,24,128]{2,1,0:T(8,128)S(1)} %add_add_fusion), kind=kLoop, calls=%fused_computation.17 | loop fusion | flops 3072 | bytes 36864 | tf_op jit(solution)/shard_map/add | solution.py:257
  (30 shorter events, 0.3 us)
Async XLA Ops:
  0.0 4.3 %copy-start = (bf16[384,2048]{1,0:T(8,128)(2,1)S(1)}, bf16[384,2048]{1,0:T(8,128)(2,1)}, u32[]{:S(2)}) copy-start(bf16[384,2048]{1,0:T(8,128)(2,1)} %param.5) | copy-start | bytes 4718596
  0.9 4.7 %collective-permute-start = (s32[9,4,8]{2,1,0:T(4,128)S(1)}, s32[9,4,8]{2,1,0:T(4,128)S(1)}, u32[]{:S(2)}, u32[]{:S(2)}) collective-permute-start(s32[9,4,8]{2,1,0:T(4,128)S(1)} %pad_add_fusion), channel_id=1, source_target_pairs={{0,8},{8,0},{1,9},{9,1},{2,10},{10,2},{3,11},{11,3},{4,12},{12,4},... | collective-permute-start | bytes 3464 | tf_op jit(solution)/shard_map/ppermute | solution.py:216
  4.3 4.3 %copy-start.1 = (bf16[8,4,8,300]{3,2,1,0:T(8,128)(2,1)S(1)}, bf16[8,4,8,300]{3,2,1,0:T(8,128)(2,1)}, u32[]{:S(2)}) copy-start(bf16[8,4,8,300]{3,2,1,0:T(8,128)(2,1)} %waves_ref.1) | copy-start | bytes 460804
  4.3 4.3 %copy-start.2 = (s32[8,4,8]{2,1,0:T(4,128)S(1)}, s32[8,4,8]{2,1,0:T(4,128)}, u32[]{:S(2)}) copy-start(s32[8,4,8]{2,1,0:T(4,128)} %shift_ref.1) | copy-start | bytes 3076
  4.3 4.3 %copy-start.3 = (s32[8,4]{0,1:T(4,128)S(1)}, s32[8,4]{0,1:T(4,128)}, u32[]{:S(2)}) copy-start(s32[8,4]{0,1:T(4,128)} %param.7) | copy-start | bytes 388
  6.3 7.2 %collective-permute-start.1 = (bf16[64,2048]{1,0:T(8,128)(2,1)S(1)}, bf16[64,2048]{1,0:T(8,128)(2,1)S(1)}, u32[]{:S(2)}, u32[]{:S(2)}) collective-permute-start(bf16[64,2048]{1,0:T(8,128)(2,1)S(1)} %convolution_convert_fusion), channel_id=1, source_target_pairs={{0,8},{8,0},{1,9},{9,1},{2,10},{10,2},{3,11},{11,3},{4,12},{12,4},... | collective-permute-start | bytes 786440 | tf_op jit(solution)/shard_map/ppermute | solution.py:224
  14.2 2.1 %collective-permute-start.3 = (f32[2,24,128]{2,1,0:T(8,128)S(1)}, f32[2,24,128]{2,1,0:T(8,128)S(1)}, u32[]{:S(2)}, u32[]{:S(2)}) collective-permute-start(f32[2,24,128]{2,1,0:T(8,128)S(1)} %stack.52), channel_id=1, source_target_pairs={{0,1},{1,0},{2,3},{3,2},{4,5},{5,4},{6,7},{7,6},{8,9},{9,8},{10,11... | collective-permute-start | bytes 73736 | tf_op jit(solution)/shard_map/ppermute | solution.py:245
  15.1 4.0 %collective-permute-start.2 = (f32[2,24,128]{2,1,0:T(8,128)S(1)}, f32[2,24,128]{2,1,0:T(8,128)S(1)}, u32[]{:S(2)}, u32[]{:S(2)}) collective-permute-start(f32[2,24,128]{2,1,0:T(8,128)S(1)} %stack.50), channel_id=1, source_target_pairs={{0,1},{1,0},{2,3},{3,2},{4,5},{5,4},{6,7},{7,6},{8,9},{9,8},{10,11... | collective-permute-start | bytes 73736 | tf_op jit(solution)/shard_map/ppermute | solution.py:245
  16.4 3.9 %collective-permute-start.4 = (f32[2,24,128]{2,1,0:T(8,128)S(1)}, f32[2,24,128]{2,1,0:T(8,128)S(1)}, u32[]{:S(2)}, u32[]{:S(2)}) collective-permute-start(f32[2,24,128]{2,1,0:T(8,128)S(1)} %add.74), channel_id=1, source_target_pairs={{0,2},{1,3},{2,0},{3,1},{4,6},{5,7},{6,4},{7,5},{8,10},{9,11},{10,... | collective-permute-start | bytes 73736 | tf_op jit(solution)/shard_map/ppermute | solution.py:245
  20.3 4.7 %collective-permute-start.5 = (f32[1,24,128]{2,1,0:T(8,128)S(1)}, f32[1,24,128]{2,1,0:T(8,128)S(1)}, u32[]{:S(2)}, u32[]{:S(2)}) collective-permute-start(f32[1,24,128]{2,1,0:T(8,128)S(1)} %slice.29), channel_id=1, source_target_pairs={{0,4},{1,5},{2,6},{3,7},{4,0},{5,1},{6,2},{7,3},{8,12},{9,13},{10,... | collective-permute-start | bytes 36872 | tf_op jit(solution)/shard_map/ppermute | solution.py:245

commit v5 on v4

--- a/solution.py
+++ b/solution.py
@@ -85,7 +85,7 @@
     tiles_ref, inv_ref, band_ref, out_ref, raw, rolled, aligned, sums, whole = refs
     taps = tiles_ref.shape[1] // LANES
     rows = len(positions) * slots
-    pitch = raw.shape[0] // rows
+    pitch = raw.shape[0] // (rows + 1)
     wide = aligned.shape[0] // rows
     for i, piece in enumerate(piece_refs):
         start = 0
@@ -165,7 +165,7 @@
         in_specs=[vmem] * (len(pieces) + 4),
         out_specs=vmem,
         scratch_shapes=[
-            pltpu.VMEM((rows * pitch, LANES), jnp.float32),
+            pltpu.VMEM(((rows + 1) * pitch, LANES), jnp.float32),
             pltpu.VMEM((rows, wide + 8, LANES), jnp.float32),
             pltpu.VMEM((rows * wide, LANES), jnp.float32),
             pltpu.VMEM((rows * wide, 2 * LANES), jnp.float32),
@@ -197,8 +197,8 @@
     count = signal.shape[0]
     wanted = of_station(groups, offsets + 1, station, stations)
     hot = wanted[..., None] == 1 + lax.broadcasted_iota(jnp.int32, (1, 1, count), 2)
-    hot = hot.reshape(templates * slots, count).astype(signal.dtype)
-    return jnp.dot(hot, signal, preferred_element_type=jnp.float32).astype(signal.dtype)
+    rows = jnp.dot(hot.astype(signal.dtype), signal, preferred_element_type=jnp.float32).astype(signal.dtype)
+    return rows.reshape(templates * slots, signal.shape[1])
 
 
 def shards(signal, waveforms, station_groups, channel_offsets, moveouts):

time: 25.8 us -> 25.7 us (level)
  transfers between devices with their start and end apart: 6 -> 6, of which waited for: 4 -> 4; matrix products, arithmetic and copies ran while one was open for 4% -> 4% of each run, Pallas kernels for 18% -> 19%
where the time goes in v5:
time: 25.7 us; the launch traced here: 25.5 us
  starting transfers between devices  10.5 us (41%)
  waiting for transfers between devices  6.33 us (25%)
  Pallas kernels  5.46 us (21%)
  other arithmetic  2 us (8%)
  matrix products  0.86 us (3%)
    ppermute x4, starting transfers between devices, across(): return lax.ppermute(x, 'stn', [(j, j ^ step) for j in range(stations)])  5.43 us
    ppermute x4, waiting for transfers between devices, across(): return lax.ppermute(x, 'stn', [(j, j ^ step) for j in range(stations)])  3.01 us
    ppermute x1, starting transfers between devices, shards(): lax.ppermute(packed, 'tmpl', swap)  2.97 us
    pallas_call x4, Pallas kernels, make_stacks(): pl.pallas_call(functools.partial(stack_kernel, slots, length, blocks, pos...  2.94 us
    pallas_call x1, Pallas kernels, make_tiles(): pl.pallas_call(functools.partial(toeplitz_kernel, slots, length, span, st...  2.52 us
    ppermute x1, waiting for transfers between devices, shards(): got = lax.ppermute(sent, 'tmpl', swap)  2.42 us
    ppermute x1, starting transfers between devices, shards(): got = lax.ppermute(sent, 'tmpl', swap)  2.09 us
    ppermute x1, waiting for transfers between devices, shards(): lax.ppermute(packed, 'tmpl', swap)  0.9 us
  transfers between devices with their start and end apart: 6, of which 4 were waited for; matrix products, arithmetic and copies ran while one was open for 4% of the time, Pallas kernels for 19%

profile of v5, /device:TPU:0, one launch (start us, length us, event | category | flops | bytes accessed | tf_op | source)
XLA Modules:
  0.0 25.5 jit_solution(4262663780947159239)
XLA Ops:
  0.0 0.9 %pad_add_fusion = s32[9,4,8]{2,1,0:T(4,128)S(1)} fusion(s32[1,4,8]{2,1,0:T(4,128)} %bitcast.29, s32[8,4,8]{2,1,0:T(4,128)} %param.8), kind=kLoop, calls=%fused_computation.19 | loop fusion | flops 288 | bytes 2304 | tf_op jit(solution)/shard_map/concatenate | solution.py:215
  0.9 3.0 %collective-permute-start = (s32[9,4,8]{2,1,0:T(4,128)S(1)}, s32[9,4,8]{2,1,0:T(4,128)S(1)}, u32[]{:S(2)}, u32[]{:S(2)}) collective-permute-start(s32[9,4,8]{2,1,0:T(4,128)S(1)} %pad_add_fusion), channel_id=1, source_target_pairs={{0,8},{8,0},{1,9},{9,1},{2,10},{10,2},{3,11},{11,3},{4,12},{12,4},... | collective-permute-start | bytes 3464 | tf_op jit(solution)/shard_map/ppermute | solution.py:216
  3.9 0.1 stack.48
  4.0 0.1 iota_compare_fusion
  4.1 0.1 select_reduce_fusion.1
  4.2 0.4 %fusion.refs_0_ = bf16[64,2048]{1,0:T(8,128)(2,1)S(1)} fusion(bf16[384,2048]{1,0:T(8,128)(2,1)S(1)} %copy-done, s32[384]{0:T(512)S(1)} %iota_add_fusion, s32[8,8]{1,0:T(8,128)S(1)} %select_reduce_fusion.1), kind=kOutput, calls=%fused_computation.2 | convolution fusion | flops 100818944 | bytes 1836800 | tf_op jit(solution)/shard_map/dot_general | solution.py:200
  4.7 0.9 %collective-permute-done = s32[9,4,8]{2,1,0:T(4,128)S(1)} collective-permute-done((s32[9,4,8]{2,1,0:T(4,128)S(1)}, s32[9,4,8]{2,1,0:T(4,128)S(1)}, u32[]{:S(2)}, u32[]{:S(2)}) %collective-permute-start) | collective-permute-done | bytes 1184 | tf_op jit(solution)/shard_map/ppermute | solution.py:216
  5.6 0.1 select_reduce_fusion
  5.7 0.4 %fusion.1 = bf16[64,2048]{1,0:T(8,128)(2,1)S(1)} fusion(bf16[384,2048]{1,0:T(8,128)(2,1)S(1)} %copy-done, s32[8,8]{1,0:T(8,128)S(1)} %select_reduce_fusion, s32[384]{0:T(512)S(1)} %iota_add_fusion), kind=kOutput, calls=%fused_computation.3 | convolution fusion | flops 100818944 | bytes 1836800 | tf_op jit(solution)/shard_map/dot_general | solution.py:200
  6.2 2.1 %collective-permute-start.1 = (bf16[64,2048]{1,0:T(8,128)(2,1)S(1)}, bf16[64,2048]{1,0:T(8,128)(2,1)S(1)}, u32[]{:S(2)}, u32[]{:S(2)}) collective-permute-start(bf16[64,2048]{1,0:T(8,128)(2,1)S(1)} %fusion.1), channel_id=1, source_target_pairs={{0,8},{8,0},{1,9},{9,1},{2,10},{10,2},{3,11},{11,3},{4,12},{12,4},... | collective-permute-start | bytes 786440 | tf_op jit(solution)/shard_map/ppermute | solution.py:224
  8.3 0.2 fusion.5.refs_4_
  8.5 2.5 %toeplitz.1 = (bf16[64,512,128]{2,1,0:T(8,128)(2,1)S(1)}, f32[64,128]{1,0:T(8,128)S(1)}, s32[8,8]{1,0:T(8,128)S(1)}) custom-call(s32[4,8]{1,0:T(4,128)S(1)} %bitcast.30, s32[8,4,8]{2,1,0:T(4,128)S(1)} %copy-done.2, bf16[8,4,8,300]{3,2,1,0:T(8,128)(2,1)S(1)} %copy-done.1), custom_call_target="tpu_custom_call" | custom-call | flops 10000000 | bytes 9000000 | tf_op jit(solution)/shard_map/toeplitz/pallas_call | solution.py:66
  11.0 2.4 %collective-permute-done.1.refs_1_ = bf16[64,2048]{1,0:T(8,128)(2,1)S(1)} collective-permute-done((bf16[64,2048]{1,0:T(8,128)(2,1)S(1)}, bf16[64,2048]{1,0:T(8,128)(2,1)S(1)}, u32[]{:S(2)}, u32[]{:S(2)}) %collective-permute-start.1) | collective-permute-done | bytes 262176 | tf_op jit(solution)/shard_map/ppermute | solution.py:224
  13.4 0.7 %stack.52 = f32[2,24,128]{2,1,0:T(8,128)S(1)} custom-call(s32[8,8]{1,0:T(8,128)S(1)} %get-tuple-element.16.scalar_ref, bf16[64,2048]{1,0:T(8,128)(2,1)S(1)} %fusion.refs_0_, bf16[64,2048]{1,0:T(8,128)(2,1)S(1)} %collective-permute-done.1.refs_1_, bf16[64,512,128]{2,1,0:T(8,128)(2,1)S(1)} %get-tuple-element.19.refs_2_, ...), custom_call_target="tpu_custom_call" | custom-call | flops 100000000 | bytes 2000000 | tf_op jit(solution)/shard_map/stack/pallas_call | solution.py:162
  14.2 0.1 collective-permute-start.3
  14.2 0.7 %stack.50 = f32[2,24,128]{2,1,0:T(8,128)S(1)} custom-call(s32[8,8]{1,0:T(8,128)S(1)} %get-tuple-element.16.scalar_ref, bf16[64,2048]{1,0:T(8,128)(2,1)S(1)} %fusion.refs_0_, bf16[64,2048]{1,0:T(8,128)(2,1)S(1)} %collective-permute-done.1.refs_1_, bf16[64,512,128]{2,1,0:T(8,128)(2,1)S(1)} %get-tuple-element.19.refs_2_, ...), custom_call_target="tpu_custom_call" | custom-call | flops 100000000 | bytes 2000000 | tf_op jit(solution)/shard_map/stack/pallas_call | solution.py:162
  15.0 0.6 %collective-permute-start.2 = (f32[2,24,128]{2,1,0:T(8,128)S(1)}, f32[2,24,128]{2,1,0:T(8,128)S(1)}, u32[]{:S(2)}, u32[]{:S(2)}) collective-permute-start(f32[2,24,128]{2,1,0:T(8,128)S(1)} %stack.50), channel_id=1, source_target_pairs={{0,1},{1,0},{2,3},{3,2},{4,5},{5,4},{6,7},{7,6},{8,9},{9,8},{10,11... | collective-permute-start | bytes 73736 | tf_op jit(solution)/shard_map/ppermute | solution.py:245
  15.5 0.7 %stack.51 = f32[2,24,128]{2,1,0:T(8,128)S(1)} custom-call(s32[8,8]{1,0:T(8,128)S(1)} %get-tuple-element.16.scalar_ref, bf16[64,2048]{1,0:T(8,128)(2,1)S(1)} %fusion.refs_0_, bf16[64,2048]{1,0:T(8,128)(2,1)S(1)} %collective-permute-done.1.refs_1_, bf16[64,512,128]{2,1,0:T(8,128)(2,1)S(1)} %get-tuple-element.19.refs_2_, ...), custom_call_target="tpu_custom_call" | custom-call | flops 100000000 | bytes 2000000 | tf_op jit(solution)/shard_map/stack/pallas_call | solution.py:162
  16.3 1.9 %collective-permute-start.4 = (f32[2,24,128]{2,1,0:T(8,128)S(1)}, f32[2,24,128]{2,1,0:T(8,128)S(1)}, u32[]{:S(2)}, u32[]{:S(2)}) collective-permute-start(f32[2,24,128]{2,1,0:T(8,128)S(1)} %add.74), channel_id=1, source_target_pairs={{0,2},{1,3},{2,0},{3,1},{4,6},{5,7},{6,4},{7,5},{8,10},{9,11},{10,... | collective-permute-start | bytes 73736 | tf_op jit(solution)/shard_map/ppermute | solution.py:245
  18.2 0.7 %stack.49 = f32[2,24,128]{2,1,0:T(8,128)S(1)} custom-call(s32[8,8]{1,0:T(8,128)S(1)} %get-tuple-element.16.scalar_ref, bf16[64,2048]{1,0:T(8,128)(2,1)S(1)} %fusion.refs_0_, bf16[64,2048]{1,0:T(8,128)(2,1)S(1)} %collective-permute-done.1.refs_1_, bf16[64,512,128]{2,1,0:T(8,128)(2,1)S(1)} %get-tuple-element.19.refs_2_, ...), custom_call_target="tpu_custom_call" | custom-call | flops 100000000 | bytes 2000000 | tf_op jit(solution)/shard_map/stack/pallas_call | solution.py:162
  18.9 1.3 %collective-permute-done.4 = f32[2,24,128]{2,1,0:T(8,128)S(1)} collective-permute-done((f32[2,24,128]{2,1,0:T(8,128)S(1)}, f32[2,24,128]{2,1,0:T(8,128)S(1)}, u32[]{:S(2)}, u32[]{:S(2)}) %collective-permute-start.4) | collective-permute-done | bytes 24608 | tf_op jit(solution)/shard_map/ppermute | solution.py:245
  20.2 2.9 %collective-permute-start.5 = (f32[1,24,128]{2,1,0:T(8,128)S(1)}, f32[1,24,128]{2,1,0:T(8,128)S(1)}, u32[]{:S(2)}, u32[]{:S(2)}) collective-permute-start(f32[1,24,128]{2,1,0:T(8,128)S(1)} %slice.29), channel_id=1, source_target_pairs={{0,4},{1,5},{2,6},{3,7},{4,0},{5,1},{6,2},{7,3},{8,12},{9,13},{10,... | collective-permute-start | bytes 36872 | tf_op jit(solution)/shard_map/ppermute | solution.py:245
  23.1 1.8 %collective-permute-done.5 = f32[1,24,128]{2,1,0:T(8,128)S(1)} collective-permute-done((f32[1,24,128]{2,1,0:T(8,128)S(1)}, f32[1,24,128]{2,1,0:T(8,128)S(1)}, u32[]{:S(2)}, u32[]{:S(2)}) %collective-permute-start.5) | collective-permute-done | bytes 12320 | tf_op jit(solution)/shard_map/ppermute | solution.py:245
  24.9 0.6 %slice_add_fusion.1 = f32[1,24,128]{2,1,0:T(8,128)} fusion(f32[1,24,128]{2,1,0:T(8,128)S(1)} %collective-permute-done.5, f32[2,24,128]{2,1,0:T(8,128)S(1)} %add_add_fusion), kind=kLoop, calls=%fused_computation.21 | loop fusion | flops 3072 | bytes 36864 | tf_op jit(solution)/shard_map/add | solution.py:257
  (28 shorter events, 0.1 us)
Async XLA Ops:
  0.0 4.2 %copy-start = (bf16[384,2048]{1,0:T(8,128)(2,1)S(1)}, bf16[384,2048]{1,0:T(8,128)(2,1)}, u32[]{:S(2)}) copy-start(bf16[384,2048]{1,0:T(8,128)(2,1)} %param.5) | copy-start | bytes 4718596
  0.9 4.7 %collective-permute-start = (s32[9,4,8]{2,1,0:T(4,128)S(1)}, s32[9,4,8]{2,1,0:T(4,128)S(1)}, u32[]{:S(2)}, u32[]{:S(2)}) collective-permute-start(s32[9,4,8]{2,1,0:T(4,128)S(1)} %pad_add_fusion), channel_id=1, source_target_pairs={{0,8},{8,0},{1,9},{9,1},{2,10},{10,2},{3,11},{11,3},{4,12},{12,4},... | collective-permute-start | bytes 3464 | tf_op jit(solution)/shard_map/ppermute | solution.py:216
  4.2 4.3 %copy-start.1 = (bf16[8,4,8,300]{3,2,1,0:T(8,128)(2,1)S(1)}, bf16[8,4,8,300]{3,2,1,0:T(8,128)(2,1)}, u32[]{:S(2)}) copy-start(bf16[8,4,8,300]{3,2,1,0:T(8,128)(2,1)} %waves_ref.1) | copy-start | bytes 460804
  4.2 4.3 %copy-start.2 = (s32[8,4,8]{2,1,0:T(4,128)S(1)}, s32[8,4,8]{2,1,0:T(4,128)}, u32[]{:S(2)}) copy-start(s32[8,4,8]{2,1,0:T(4,128)} %shift_ref.1) | copy-start | bytes 3076
  4.2 4.3 %copy-start.3 = (s32[8,4]{0,1:T(4,128)S(1)}, s32[8,4]{0,1:T(4,128)}, u32[]{:S(2)}) copy-start(s32[8,4]{0,1:T(4,128)} %param.7) | copy-start | bytes 388
  6.2 7.2 %collective-permute-start.1 = (bf16[64,2048]{1,0:T(8,128)(2,1)S(1)}, bf16[64,2048]{1,0:T(8,128)(2,1)S(1)}, u32[]{:S(2)}, u32[]{:S(2)}) collective-permute-start(bf16[64,2048]{1,0:T(8,128)(2,1)S(1)} %fusion.1), channel_id=1, source_target_pairs={{0,8},{8,0},{1,9},{9,1},{2,10},{10,2},{3,11},{11,3},{4,12},{12,4},... | collective-permute-start | bytes 786440 | tf_op jit(solution)/shard_map/ppermute | solution.py:224
  14.2 2.1 %collective-permute-start.3 = (f32[2,24,128]{2,1,0:T(8,128)S(1)}, f32[2,24,128]{2,1,0:T(8,128)S(1)}, u32[]{:S(2)}, u32[]{:S(2)}) collective-permute-start(f32[2,24,128]{2,1,0:T(8,128)S(1)} %stack.52), channel_id=1, source_target_pairs={{0,1},{1,0},{2,3},{3,2},{4,5},{5,4},{6,7},{7,6},{8,9},{9,8},{10,11... | collective-permute-start | bytes 73736 | tf_op jit(solution)/shard_map/ppermute | solution.py:245
  15.0 4.0 %collective-permute-start.2 = (f32[2,24,128]{2,1,0:T(8,128)S(1)}, f32[2,24,128]{2,1,0:T(8,128)S(1)}, u32[]{:S(2)}, u32[]{:S(2)}) collective-permute-start(f32[2,24,128]{2,1,0:T(8,128)S(1)} %stack.50), channel_id=1, source_target_pairs={{0,1},{1,0},{2,3},{3,2},{4,5},{5,4},{6,7},{7,6},{8,9},{9,8},{10,11... | collective-permute-start | bytes 73736 | tf_op jit(solution)/shard_map/ppermute | solution.py:245
  16.3 3.9 %collective-permute-start.4 = (f32[2,24,128]{2,1,0:T(8,128)S(1)}, f32[2,24,128]{2,1,0:T(8,128)S(1)}, u32[]{:S(2)}, u32[]{:S(2)}) collective-permute-start(f32[2,24,128]{2,1,0:T(8,128)S(1)} %add.74), channel_id=1, source_target_pairs={{0,2},{1,3},{2,0},{3,1},{4,6},{5,7},{6,4},{7,5},{8,10},{9,11},{10,... | collective-permute-start | bytes 73736 | tf_op jit(solution)/shard_map/ppermute | solution.py:245
  20.2 4.7 %collective-permute-start.5 = (f32[1,24,128]{2,1,0:T(8,128)S(1)}, f32[1,24,128]{2,1,0:T(8,128)S(1)}, u32[]{:S(2)}, u32[]{:S(2)}) collective-permute-start(f32[1,24,128]{2,1,0:T(8,128)S(1)} %slice.29), channel_id=1, source_target_pairs={{0,4},{1,5},{2,6},{3,7},{4,0},{5,1},{6,2},{7,3},{8,12},{9,13},{10,... | collective-permute-start | bytes 36872 | tf_op jit(solution)/shard_map/ppermute | solution.py:245
